TPU v7x, 512 devices: a whole 4x4x16 slice. The times are simulated.
512 devices in a mesh: gz: 16 (over y, x), pa: 32 (over z, core).
Axes of the slice: x: 4, y: 4, z: 16, core: 2. Of those that a mesh axis runs over, the one named last changes fastest.
Arguments:
- particles: float32 [6, 1048576], P(None, ('gz', 'pa')), may hold values from -6 to 6
- slice_index: int32 [1048576], P(('gz', 'pa')), may hold values from 0 to 127
- moving: int32 [16, 32, 2], P('gz', 'pa'), may hold values from 0 to 384, as said below
- decay_rate: float32 [8], replicated, may hold values from 0.3 to 600
- wake_freq: float32 [8], replicated, may hold values from -3.140625 to 3.140625
- wake_amp: float32 [4, 8], replicated, may hold values from -3 to 3
Outputs:
- wake_kick: float32 [3, 2048], P(None, 'gz')
- particles_out: float32 [6, 1441792], P(None, ('gz', 'pa'))
Inputs may be any that keep to these rules, and one draw needn't show every extreme that they name: `moving`: each entry is at most 384, and some entry equals 384.
All inputs are finite; a program needn't handle non-finite values.
Results may differ from a plain program's by a relative error of at most 0.0003.
Values sent between devices are 32-bit elements; how exact they have to be, the bound alone decides.
No kernel may reach another device: no remote copies, remote signals or barrier semaphores. Data moves between devices by JAX's collectives and lax.ppermute only.
A program may use at most 64 MiB of HBM per device.

v0:
```python
import math

import jax
import jax.numpy as jnp
from jax import lax
from jax.sharding import PartitionSpec as P

S_DEV = 128


two_pi = 6.283185307179586
adjust_horiz = 0.269
adjust_vert = 0.355
chroma_horiz = 0.05
chroma_vert = 0.04
curve_horiz = 0.02
curve_vert = -0.015
detune_self = 0.03
detune_cross = -0.02
voltage = 0.05
synch_phase = 0.3
slippage = 0.1


def from_behind_2(value, axis, steps):
    count = lax.axis_size(axis)
    leading, last = (max(0, -steps), min(count, count - steps))
    return lax.ppermute(value, axis, [(source, source + steps) for source in range(leading, last)])


def complex_mul(first, second):
    return jnp.stack(
        [first[0] * second[0] - first[1] * second[1], first[0] * second[1] + first[1] * second[0]]
    )


def powers(damping, wake_freq, distance):
    envelope = jnp.exp(-damping[:, None] * distance[None, :])
    angles = wake_freq[:, None] * distance[None, :]
    return (envelope * jnp.cos(angles), envelope * jnp.sin(angles))


def toeplitz(wave):
    slab_width = wave.shape[0]
    row_index = lax.broadcasted_iota(jnp.int32, (slab_width, slab_width), 0)
    col_index = lax.broadcasted_iota(jnp.int32, (slab_width, slab_width), 1)
    offset = col_index - row_index
    picked = jnp.take(wave, jnp.clip(offset, 0, slab_width - 1))
    return jnp.where(offset > 0, picked, jnp.float32(0.0))


def slab_tables(decay_rate, wake_freq, wake_amp, slab_width, slice_total):
    damping = decay_rate / slice_total
    norm_trans = jnp.sqrt(2.0 * damping)
    norm_long = jnp.sqrt(damping * damping + wake_freq * wake_freq)
    coef_real = jnp.stack(
        [wake_amp[0] * norm_trans, wake_amp[0] * norm_trans, wake_amp[2] * norm_long], axis=1
    )
    coef_imag = jnp.stack(
        [wake_amp[1] * norm_trans, wake_amp[1] * norm_trans, wake_amp[3] * norm_long], axis=1
    )
    distance = jnp.arange(slab_width, dtype=jnp.float32)
    near_re, near_im = powers(damping, wake_freq, distance)
    far_re, far_im = powers(damping, wake_freq, slab_width - distance)
    whole_re, whole_im = powers(damping, wake_freq, jnp.full((1,), slab_width, jnp.float32))
    factor = jnp.stack(
        [jnp.broadcast_to(whole_re, coef_real.shape), jnp.broadcast_to(whole_im, coef_real.shape)]
    )
    wave_trans = jnp.sum(
        norm_trans[:, None] * (wake_amp[0][:, None] * near_re - wake_amp[1][:, None] * near_im),
        axis=0,
    )
    wave_long = jnp.sum(
        norm_long[:, None] * (wake_amp[2][:, None] * near_re - wake_amp[3][:, None] * near_im),
        axis=0,
    )
    return (
        toeplitz(wave_trans),
        toeplitz(wave_long),
        near_re,
        near_im,
        far_re,
        far_im,
        factor,
        coef_real,
        coef_imag,
    )


def slab_summary(moments, tables):
    highest = lax.Precision.HIGHEST
    return jnp.stack(
        [
            jnp.dot(tables[4], moments.T, precision=highest),
            jnp.dot(tables[5], moments.T, precision=highest),
        ]
    )


def slab_kick(moments, carried, tables):
    highest = lax.Precision.HIGHEST
    trans_kick = jnp.dot(moments[0:2], tables[0], precision=highest)
    long_kick = jnp.dot(moments[2:3], tables[1], precision=highest)
    coef_re = tables[7] * carried[0] - tables[8] * carried[1]
    coef_im = tables[7] * carried[1] + tables[8] * carried[0]
    incoming = jnp.dot(coef_re.T, tables[2], precision=highest) - jnp.dot(
        coef_im.T, tables[3], precision=highest
    )
    return jnp.concatenate([trans_kick, long_kick], axis=0) + incoming


def moment_values(particles, mean_fill):
    root_fill = math.sqrt(mean_fill)
    return jnp.stack(
        [
            particles[0] / root_fill,
            particles[2] / root_fill,
            jnp.full_like(particles[0], 1.0 / mean_fill),
        ]
    )


def deposit(values, index, segments):
    return jax.vmap(lambda column: jax.ops.segment_sum(column, index, num_segments=segments))(
        values
    )


def one_turn(coords, kicks):
    hor_pos = coords[0]
    hor_mom = coords[1] + kicks[0]
    ver_pos = coords[2]
    ver_mom = coords[3] + kicks[1]
    lag_pos = coords[4]
    energy_dev = coords[5] + kicks[2]
    action_x = 0.5 * (hor_pos * hor_pos + hor_mom * hor_mom)
    action_y = 0.5 * (ver_pos * ver_pos + ver_mom * ver_mom)
    phase_x = two_pi * (
        adjust_horiz
        + chroma_horiz * energy_dev
        + curve_horiz * energy_dev * energy_dev
        + detune_self * action_x
        + detune_cross * action_y
    )
    phase_y = two_pi * (
        adjust_vert
        + chroma_vert * energy_dev
        + curve_vert * energy_dev * energy_dev
        + detune_self * action_y
        + detune_cross * action_x
    )
    cosine_x = jnp.cos(phase_x)
    sine_x = jnp.sin(phase_x)
    cosine_y = jnp.cos(phase_y)
    sine_y = jnp.sin(phase_y)
    new_energy = energy_dev - voltage * (jnp.sin(synch_phase + lag_pos) - math.sin(synch_phase))
    new_lag = lag_pos - slippage * new_energy
    return jnp.stack(
        [
            cosine_x * hor_pos + sine_x * hor_mom,
            cosine_x * hor_mom - sine_x * hor_pos,
            cosine_y * ver_pos + sine_y * ver_mom,
            cosine_y * ver_mom - sine_y * ver_pos,
            new_lag,
            new_energy,
        ]
    )


def upstream(own_summary, factor, slab_count):

    def advance(step_index, carried):
        return from_behind_2(complex_mul(factor, carried) + own_summary, "gz", 1)

    return lax.fori_loop(0, slab_count - 1, advance, jnp.zeros_like(own_summary))


def body(particles, slice_index, moving, decay_rate, wake_freq, wake_amp):
    slab_count = lax.axis_size("gz")
    member_count = lax.axis_size("pa")
    local_count = particles.shape[1]
    slab_width = S_DEV
    tables = slab_tables(decay_rate, wake_freq, wake_amp, slab_width, slab_width * slab_count)
    mean_fill = local_count * member_count / slab_width
    values = moment_values(particles, mean_fill)
    partial_moments = deposit(values, slice_index, slab_width)
    moments = lax.psum(partial_moments, "pa")
    carried = upstream(slab_summary(moments, tables), tables[6], slab_count)
    wake_kick = slab_kick(moments, carried, tables)
    per_particle = jnp.take(wake_kick, slice_index, axis=1)
    capacity = local_count * 3 // 16
    head_count = moving[0, 0, 0]
    tail_count = moving[0, 0, 1]
    slot_index = lax.broadcasted_iota(jnp.int32, (1, capacity), 1)
    leaving_head = slot_index < head_count
    leaving_tail = slot_index >= capacity - tail_count
    zero_value = jnp.float32(0.0)
    tail_start = local_count - capacity
    moved_all = one_turn(particles, per_particle)
    head_part = moved_all[:, :capacity]
    tail_part = moved_all[:, tail_start:]
    head_send = jnp.where(leaving_head, head_part, zero_value)
    tail_send = jnp.where(leaving_tail, tail_part, zero_value)
    from_behind = from_behind_2(head_send, "gz", -1)
    from_ahead = from_behind_2(tail_send, "gz", 1)
    head_kept = jnp.where(leaving_head, zero_value, head_part)
    tail_kept = jnp.where(leaving_tail, zero_value, tail_part)
    middle_part = moved_all[:, capacity:tail_start]
    particles_out = jnp.concatenate(
        [from_behind, head_kept, middle_part, tail_kept, from_ahead], axis=1
    )
    return (wake_kick, particles_out)


def solution(mesh):
    return jax.shard_map(
        body,
        mesh=mesh,
        in_specs=(P(None, ("gz", "pa")), P(("gz", "pa")), P("gz", "pa", None), P(), P(), P()),
        out_specs=(P(None, "gz"), P(None, ("gz", "pa"))),
        check_vma=False,
    )
```

profile of v0, /device:TPU:16, one launch (start us, length us, event | category | flops | bytes accessed | tf_op | source)
XLA Modules:
  0.0 447.7 jit_solution(7515340950392063301)
XLA Ops:
  2.4 11.5 %scatter_custom_fusion = f32[3,128]{0,1:T(8,128)S(1)} fusion(s32[2048]{0:T(1024)S(1)} %copy-done.1, f32[2048,3]{1,0:T(8,128)S(1)} %copy.80, f32[]{:T(128)} %constant.22.clone.1), kind=kCustom, calls=%fused_computation.37 | custom fusion | flops 6144 | bytes 1540 | tf_op jit(solution)/shard_map/vmap()/scatter-add | solution.py:124
  14.0 99.1 %psum.7 = f32[3,128]{0,1:T(8,128)S(1)} all-reduce(f32[3,128]{0,1:T(8,128)S(1)} %scatter_custom_fusion), channel_id=1, replica_groups=mesh['gz'=16,'pa'=32] {'pa'}, use_global_device_ids=true, to_apply=%region_1.0 | all-reduce | flops 384 | bytes 3072 | tf_op jit(solution)/shard_map/psum | solution.py:187
  113.9 114.3 %while.11 = (s32[]{:T(128)}, f32[2,8,3]{1,0,2:T(2,128)S(1)}, f32[2,8,3]{1,0,2:T(2,128)S(1)}, f32[8]{0:T(128)S(1)}, f32[8]{0:T(128)S(1)}, /*index=5*/s32[]{:T(128)}) while((s32[]{:T(128)}, f32[2,8,3]{1,0,2:T(2,128)S(1)}, f32[2,8,3]{1,0,2:T(2,128)S(1)}, f32[8]{0:T(128)S(1)}, f32[8]{0:T(128)S(1)}, /*index=5*/s32[]{:T(128)}) %tuple.64), condition=%wide.region_5.7_spmd.clone, body=%wide.region_4.6_spmd.clone.sunk | while | flops 242 | bytes 1901 | solution.py:175
  113.9 3.4 collective-permute-start
  117.4 4.2 collective-permute-done
  121.6 1.9 collective-permute-start
  123.5 5.7 %collective-permute-done = f32[2,8,3]{1,0,2:T(2,128)S(1)} collective-permute-done((f32[2,8,3]{1,0,2:T(2,128)S(1)}, f32[2,8,3]{1,0,2:T(2,128)S(1)}, u32[]{:S(2)}, u32[]{:S(2)}) %collective-permute-start) | collective-permute-done | bytes 224 | tf_op jit(solution)/shard_map/while/body/eval_jaxpr/ppermute | solution.py:28
  129.2 1.9 collective-permute-start
  131.1 5.7 %collective-permute-done = f32[2,8,3]{1,0,2:T(2,128)S(1)} collective-permute-done((f32[2,8,3]{1,0,2:T(2,128)S(1)}, f32[2,8,3]{1,0,2:T(2,128)S(1)}, u32[]{:S(2)}, u32[]{:S(2)}) %collective-permute-start) | collective-permute-done | bytes 224 | tf_op jit(solution)/shard_map/while/body/eval_jaxpr/ppermute | solution.py:28
  136.8 1.9 collective-permute-start
  138.7 5.7 %collective-permute-done = f32[2,8,3]{1,0,2:T(2,128)S(1)} collective-permute-done((f32[2,8,3]{1,0,2:T(2,128)S(1)}, f32[2,8,3]{1,0,2:T(2,128)S(1)}, u32[]{:S(2)}, u32[]{:S(2)}) %collective-permute-start) | collective-permute-done | bytes 224 | tf_op jit(solution)/shard_map/while/body/eval_jaxpr/ppermute | solution.py:28
  144.4 1.9 collective-permute-start
  146.4 5.7 %collective-permute-done = f32[2,8,3]{1,0,2:T(2,128)S(1)} collective-permute-done((f32[2,8,3]{1,0,2:T(2,128)S(1)}, f32[2,8,3]{1,0,2:T(2,128)S(1)}, u32[]{:S(2)}, u32[]{:S(2)}) %collective-permute-start) | collective-permute-done | bytes 224 | tf_op jit(solution)/shard_map/while/body/eval_jaxpr/ppermute | solution.py:28
  152.0 1.9 collective-permute-start
  154.0 5.7 %collective-permute-done = f32[2,8,3]{1,0,2:T(2,128)S(1)} collective-permute-done((f32[2,8,3]{1,0,2:T(2,128)S(1)}, f32[2,8,3]{1,0,2:T(2,128)S(1)}, u32[]{:S(2)}, u32[]{:S(2)}) %collective-permute-start) | collective-permute-done | bytes 224 | tf_op jit(solution)/shard_map/while/body/eval_jaxpr/ppermute | solution.py:28
  159.7 1.9 collective-permute-start
  161.6 5.7 %collective-permute-done = f32[2,8,3]{1,0,2:T(2,128)S(1)} collective-permute-done((f32[2,8,3]{1,0,2:T(2,128)S(1)}, f32[2,8,3]{1,0,2:T(2,128)S(1)}, u32[]{:S(2)}, u32[]{:S(2)}) %collective-permute-start) | collective-permute-done | bytes 224 | tf_op jit(solution)/shard_map/while/body/eval_jaxpr/ppermute | solution.py:28
  169.2 5.7 %collective-permute-done = f32[2,8,3]{1,0,2:T(2,128)S(1)} collective-permute-done((f32[2,8,3]{1,0,2:T(2,128)S(1)}, f32[2,8,3]{1,0,2:T(2,128)S(1)}, u32[]{:S(2)}, u32[]{:S(2)}) %collective-permute-start) | collective-permute-done | bytes 224 | tf_op jit(solution)/shard_map/while/body/eval_jaxpr/ppermute | solution.py:28
  176.8 5.7 %collective-permute-done = f32[2,8,3]{1,0,2:T(2,128)S(1)} collective-permute-done((f32[2,8,3]{1,0,2:T(2,128)S(1)}, f32[2,8,3]{1,0,2:T(2,128)S(1)}, u32[]{:S(2)}, u32[]{:S(2)}) %collective-permute-start) | collective-permute-done | bytes 224 | tf_op jit(solution)/shard_map/while/body/eval_jaxpr/ppermute | solution.py:28
  184.5 5.7 %collective-permute-done = f32[2,8,3]{1,0,2:T(2,128)S(1)} collective-permute-done((f32[2,8,3]{1,0,2:T(2,128)S(1)}, f32[2,8,3]{1,0,2:T(2,128)S(1)}, u32[]{:S(2)}, u32[]{:S(2)}) %collective-permute-start) | collective-permute-done | bytes 224 | tf_op jit(solution)/shard_map/while/body/eval_jaxpr/ppermute | solution.py:28
  192.1 5.7 %collective-permute-done = f32[2,8,3]{1,0,2:T(2,128)S(1)} collective-permute-done((f32[2,8,3]{1,0,2:T(2,128)S(1)}, f32[2,8,3]{1,0,2:T(2,128)S(1)}, u32[]{:S(2)}, u32[]{:S(2)}) %collective-permute-start) | collective-permute-done | bytes 224 | tf_op jit(solution)/shard_map/while/body/eval_jaxpr/ppermute | solution.py:28
  199.7 5.7 %collective-permute-done = f32[2,8,3]{1,0,2:T(2,128)S(1)} collective-permute-done((f32[2,8,3]{1,0,2:T(2,128)S(1)}, f32[2,8,3]{1,0,2:T(2,128)S(1)}, u32[]{:S(2)}, u32[]{:S(2)}) %collective-permute-start) | collective-permute-done | bytes 224 | tf_op jit(solution)/shard_map/while/body/eval_jaxpr/ppermute | solution.py:28
  207.3 5.7 %collective-permute-done = f32[2,8,3]{1,0,2:T(2,128)S(1)} collective-permute-done((f32[2,8,3]{1,0,2:T(2,128)S(1)}, f32[2,8,3]{1,0,2:T(2,128)S(1)}, u32[]{:S(2)}, u32[]{:S(2)}) %collective-permute-start) | collective-permute-done | bytes 224 | tf_op jit(solution)/shard_map/while/body/eval_jaxpr/ppermute | solution.py:28
  214.9 5.7 %collective-permute-done = f32[2,8,3]{1,0,2:T(2,128)S(1)} collective-permute-done((f32[2,8,3]{1,0,2:T(2,128)S(1)}, f32[2,8,3]{1,0,2:T(2,128)S(1)}, u32[]{:S(2)}, u32[]{:S(2)}) %collective-permute-start) | collective-permute-done | bytes 224 | tf_op jit(solution)/shard_map/while/body/eval_jaxpr/ppermute | solution.py:28
  222.6 5.7 %collective-permute-done = f32[2,8,3]{1,0,2:T(2,128)S(1)} collective-permute-done((f32[2,8,3]{1,0,2:T(2,128)S(1)}, f32[2,8,3]{1,0,2:T(2,128)S(1)}, u32[]{:S(2)}, u32[]{:S(2)}) %collective-permute-start) | collective-permute-done | bytes 224 | tf_op jit(solution)/shard_map/while/body/eval_jaxpr/ppermute | solution.py:28
  228.4 97.2 %gather_fusion.1 = f32[16384]{0:T(1024)S(1)} fusion(f32[128]{0:T(128)S(1)} %get-tuple-element.75, s32[16384]{0:T(1024)S(1)} %bitcast_clamp_fusion), kind=kCustom, calls=%fused_computation.clone | custom fusion | bytes 196608 | tf_op jit(solution)/shard_map/jit(_take)/gather | solution.py:48
  325.8 97.2 %gather_fusion.2 = f32[16384]{0:T(1024)S(1)} fusion(f32[128]{0:T(128)S(1)} %get-tuple-element.76, s32[16384]{0:T(1024)S(1)} %bitcast_clamp_fusion), kind=kCustom, calls=%fused_computation.1.clone | custom fusion | bytes 196608 | tf_op jit(solution)/shard_map/jit(_take)/gather | solution.py:48
  424.3 5.5 %gather_fusion = f32[2048,3]{1,0:T(8,128)S(1)} fusion(f32[3,128]{0,1:T(8,128)S(1)} %copy.82, s32[2048]{0:T(1024)S(1)} %fusion.32), kind=kCustom, calls=%fused_computation.2 | custom fusion | bytes 57344 | tf_op jit(solution)/shard_map/jit(_take)/gather | solution.py:190
  433.7 1.9 collective-permute-start.1
  436.3 3.0 collective-permute-done.1
  439.4 1.9 collective-permute-start.2
  441.3 5.8 %collective-permute-done.2 = f32[6,384]{1,0:T(8,128)S(1)} collective-permute-done((f32[6,384]{1,0:T(8,128)S(1)}, f32[6,384]{1,0:T(8,128)S(1)}, u32[]{:S(2)}, u32[]{:S(2)}) %collective-permute-start.2) | collective-permute-done | bytes 9248 | tf_op jit(solution)/shard_map/ppermute | solution.py:28
  (93 shorter events, 24.5 us)
Async XLA Ops:
  1.7 0.7 copy-start.1
  13.9 99.1 %copy-start.2 = (f32[4,8]{1,0:T(4,128)S(1)}, f32[4,8]{1,0:T(4,128)}, u32[]{:S(2)}) copy-start(f32[4,8]{1,0:T(4,128)} %param.15) | copy-start | bytes 388
  13.9 99.1 %copy-start.6 = (f32[8]{0:T(128)S(1)}, f32[8]{0:T(128)}, u32[]{:S(2)}) copy-start(f32[8]{0:T(128)} %param.13) | copy-start | bytes 100
  13.9 99.1 %copy-start.7 = (f32[8]{0:T(128)S(1)}, f32[8]{0:T(128)}, u32[]{:S(2)}) copy-start(f32[8]{0:T(128)} %param.14) | copy-start | bytes 100
  113.9 7.6 %collective-permute-start = (f32[2,8,3]{1,0,2:T(2,128)S(1)}, f32[2,8,3]{1,0,2:T(2,128)S(1)}, u32[]{:S(2)}, u32[]{:S(2)}) collective-permute-start(f32[2,8,3]{1,0,2:T(2,128)S(1)} %maximum_add_fusion.2), channel_id=1, source_target_pairs={{0,32},{32,64},{64,96},{96,128},{128,160},{160,192},{192,224},{224... | collective-permute-start | bytes 584 | tf_op jit(solution)/shard_map/while/body/eval_jaxpr/ppermute | solution.py:28
  121.6 7.6 %collective-permute-start = (f32[2,8,3]{1,0,2:T(2,128)S(1)}, f32[2,8,3]{1,0,2:T(2,128)S(1)}, u32[]{:S(2)}, u32[]{:S(2)}) collective-permute-start(f32[2,8,3]{1,0,2:T(2,128)S(1)} %maximum_add_fusion.2), channel_id=1, source_target_pairs={{0,32},{32,64},{64,96},{96,128},{128,160},{160,192},{192,224},{224... | collective-permute-start | bytes 584 | tf_op jit(solution)/shard_map/while/body/eval_jaxpr/ppermute | solution.py:28
  129.2 7.6 %collective-permute-start = (f32[2,8,3]{1,0,2:T(2,128)S(1)}, f32[2,8,3]{1,0,2:T(2,128)S(1)}, u32[]{:S(2)}, u32[]{:S(2)}) collective-permute-start(f32[2,8,3]{1,0,2:T(2,128)S(1)} %maximum_add_fusion.2), channel_id=1, source_target_pairs={{0,32},{32,64},{64,96},{96,128},{128,160},{160,192},{192,224},{224... | collective-permute-start | bytes 584 | tf_op jit(solution)/shard_map/while/body/eval_jaxpr/ppermute | solution.py:28
  136.8 7.6 %collective-permute-start = (f32[2,8,3]{1,0,2:T(2,128)S(1)}, f32[2,8,3]{1,0,2:T(2,128)S(1)}, u32[]{:S(2)}, u32[]{:S(2)}) collective-permute-start(f32[2,8,3]{1,0,2:T(2,128)S(1)} %maximum_add_fusion.2), channel_id=1, source_target_pairs={{0,32},{32,64},{64,96},{96,128},{128,160},{160,192},{192,224},{224... | collective-permute-start | bytes 584 | tf_op jit(solution)/shard_map/while/body/eval_jaxpr/ppermute | solution.py:28
  144.4 7.6 %collective-permute-start = (f32[2,8,3]{1,0,2:T(2,128)S(1)}, f32[2,8,3]{1,0,2:T(2,128)S(1)}, u32[]{:S(2)}, u32[]{:S(2)}) collective-permute-start(f32[2,8,3]{1,0,2:T(2,128)S(1)} %maximum_add_fusion.2), channel_id=1, source_target_pairs={{0,32},{32,64},{64,96},{96,128},{128,160},{160,192},{192,224},{224... | collective-permute-start | bytes 584 | tf_op jit(solution)/shard_map/while/body/eval_jaxpr/ppermute | solution.py:28
  152.0 7.6 %collective-permute-start = (f32[2,8,3]{1,0,2:T(2,128)S(1)}, f32[2,8,3]{1,0,2:T(2,128)S(1)}, u32[]{:S(2)}, u32[]{:S(2)}) collective-permute-start(f32[2,8,3]{1,0,2:T(2,128)S(1)} %maximum_add_fusion.2), channel_id=1, source_target_pairs={{0,32},{32,64},{64,96},{96,128},{128,160},{160,192},{192,224},{224... | collective-permute-start | bytes 584 | tf_op jit(solution)/shard_map/while/body/eval_jaxpr/ppermute | solution.py:28
  159.7 7.6 %collective-permute-start = (f32[2,8,3]{1,0,2:T(2,128)S(1)}, f32[2,8,3]{1,0,2:T(2,128)S(1)}, u32[]{:S(2)}, u32[]{:S(2)}) collective-permute-start(f32[2,8,3]{1,0,2:T(2,128)S(1)} %maximum_add_fusion.2), channel_id=1, source_target_pairs={{0,32},{32,64},{64,96},{96,128},{128,160},{160,192},{192,224},{224... | collective-permute-start | bytes 584 | tf_op jit(solution)/shard_map/while/body/eval_jaxpr/ppermute | solution.py:28
  167.3 7.6 %collective-permute-start = (f32[2,8,3]{1,0,2:T(2,128)S(1)}, f32[2,8,3]{1,0,2:T(2,128)S(1)}, u32[]{:S(2)}, u32[]{:S(2)}) collective-permute-start(f32[2,8,3]{1,0,2:T(2,128)S(1)} %maximum_add_fusion.2), channel_id=1, source_target_pairs={{0,32},{32,64},{64,96},{96,128},{128,160},{160,192},{192,224},{224... | collective-permute-start | bytes 584 | tf_op jit(solution)/shard_map/while/body/eval_jaxpr/ppermute | solution.py:28
  174.9 7.6 %collective-permute-start = (f32[2,8,3]{1,0,2:T(2,128)S(1)}, f32[2,8,3]{1,0,2:T(2,128)S(1)}, u32[]{:S(2)}, u32[]{:S(2)}) collective-permute-start(f32[2,8,3]{1,0,2:T(2,128)S(1)} %maximum_add_fusion.2), channel_id=1, source_target_pairs={{0,32},{32,64},{64,96},{96,128},{128,160},{160,192},{192,224},{224... | collective-permute-start | bytes 584 | tf_op jit(solution)/shard_map/while/body/eval_jaxpr/ppermute | solution.py:28
  182.5 7.6 %collective-permute-start = (f32[2,8,3]{1,0,2:T(2,128)S(1)}, f32[2,8,3]{1,0,2:T(2,128)S(1)}, u32[]{:S(2)}, u32[]{:S(2)}) collective-permute-start(f32[2,8,3]{1,0,2:T(2,128)S(1)} %maximum_add_fusion.2), channel_id=1, source_target_pairs={{0,32},{32,64},{64,96},{96,128},{128,160},{160,192},{192,224},{224... | collective-permute-start | bytes 584 | tf_op jit(solution)/shard_map/while/body/eval_jaxpr/ppermute | solution.py:28
  190.2 7.6 %collective-permute-start = (f32[2,8,3]{1,0,2:T(2,128)S(1)}, f32[2,8,3]{1,0,2:T(2,128)S(1)}, u32[]{:S(2)}, u32[]{:S(2)}) collective-permute-start(f32[2,8,3]{1,0,2:T(2,128)S(1)} %maximum_add_fusion.2), channel_id=1, source_target_pairs={{0,32},{32,64},{64,96},{96,128},{128,160},{160,192},{192,224},{224... | collective-permute-start | bytes 584 | tf_op jit(solution)/shard_map/while/body/eval_jaxpr/ppermute | solution.py:28
  197.8 7.6 %collective-permute-start = (f32[2,8,3]{1,0,2:T(2,128)S(1)}, f32[2,8,3]{1,0,2:T(2,128)S(1)}, u32[]{:S(2)}, u32[]{:S(2)}) collective-permute-start(f32[2,8,3]{1,0,2:T(2,128)S(1)} %maximum_add_fusion.2), channel_id=1, source_target_pairs={{0,32},{32,64},{64,96},{96,128},{128,160},{160,192},{192,224},{224... | collective-permute-start | bytes 584 | tf_op jit(solution)/shard_map/while/body/eval_jaxpr/ppermute | solution.py:28
  205.4 7.6 %collective-permute-start = (f32[2,8,3]{1,0,2:T(2,128)S(1)}, f32[2,8,3]{1,0,2:T(2,128)S(1)}, u32[]{:S(2)}, u32[]{:S(2)}) collective-permute-start(f32[2,8,3]{1,0,2:T(2,128)S(1)} %maximum_add_fusion.2), channel_id=1, source_target_pairs={{0,32},{32,64},{64,96},{96,128},{128,160},{160,192},{192,224},{224... | collective-permute-start | bytes 584 | tf_op jit(solution)/shard_map/while/body/eval_jaxpr/ppermute | solution.py:28
  213.0 7.6 %collective-permute-start = (f32[2,8,3]{1,0,2:T(2,128)S(1)}, f32[2,8,3]{1,0,2:T(2,128)S(1)}, u32[]{:S(2)}, u32[]{:S(2)}) collective-permute-start(f32[2,8,3]{1,0,2:T(2,128)S(1)} %maximum_add_fusion.2), channel_id=1, source_target_pairs={{0,32},{32,64},{64,96},{96,128},{128,160},{160,192},{192,224},{224... | collective-permute-start | bytes 584 | tf_op jit(solution)/shard_map/while/body/eval_jaxpr/ppermute | solution.py:28
  220.6 7.6 %collective-permute-start = (f32[2,8,3]{1,0,2:T(2,128)S(1)}, f32[2,8,3]{1,0,2:T(2,128)S(1)}, u32[]{:S(2)}, u32[]{:S(2)}) collective-permute-start(f32[2,8,3]{1,0,2:T(2,128)S(1)} %maximum_add_fusion.2), channel_id=1, source_target_pairs={{0,32},{32,64},{64,96},{96,128},{128,160},{160,192},{192,224},{224... | collective-permute-start | bytes 584 | tf_op jit(solution)/shard_map/while/body/eval_jaxpr/ppermute | solution.py:28
  423.7 0.6 copy-start.3
  430.1 0.9 copy-start
  431.0 0.7 copy-start.4
  433.7 5.6 %collective-permute-start.1 = (f32[6,384]{1,0:T(8,128)S(1)}, f32[6,384]{1,0:T(8,128)S(1)}, u32[]{:S(2)}, u32[]{:S(2)}) collective-permute-start(f32[6,384]{1,0:T(8,128)S(1)} %slice_select_fusion.1), channel_id=1, source_target_pairs={{32,0},{64,32},{96,64},{128,96},{160,128},{192,160},{224,192},{256... | collective-permute-start | bytes 27656 | tf_op jit(solution)/shard_map/ppermute | solution.py:28
  439.4 7.7 %collective-permute-start.2 = (f32[6,384]{1,0:T(8,128)S(1)}, f32[6,384]{1,0:T(8,128)S(1)}, u32[]{:S(2)}, u32[]{:S(2)}) collective-permute-start(f32[6,384]{1,0:T(8,128)S(1)} %get-tuple-element.109), channel_id=1, source_target_pairs={{0,32},{32,64},{64,96},{96,128},{128,160},{160,192},{192,224},{224... | collective-permute-start | bytes 27656 | tf_op jit(solution)/shard_map/ppermute | solution.py:28
  447.1 0.6 copy-start.5
where the time goes:
time: 450 us; the launch traced here: 448 us
  local copies, waits for them, and re-layouts  204 us (45%)
  blocking collectives  99.1 us (22%)
  waiting for transfers between devices  92.3 us (21%)
  starting transfers between devices  34.1 us (8%)
  other arithmetic  15 us (3%)
    gather x2, local copies, waits for them, and re-layouts, toeplitz(): picked = jnp.take(wave, jnp.clip(offset, 0, slab_width - 1))  194 us
    psum x1, blocking collectives, body(): moments = lax.psum(partial_moments, 'pa')  99.1 us
    ppermute x17, waiting for transfers between devices, from_behind_2(): lax.ppermute(value, axis, [(source, source + steps) for source in range(l...  92.3 us
    ppermute x17, starting transfers between devices, from_behind_2(): lax.ppermute(value, axis, [(source, source + steps) for source in range(l...  34.1 us
    scatter-add x1, other arithmetic, deposit(): jax.ops.segment_sum(column, index, num_segments=segments)  11.5 us
  transfers between devices with their start and end apart: 17, of which 17 were waited for; matrix products, arithmetic and copies ran while one was open for 0% of the time, Pallas kernels for 0%

commit v1 on v0

v1 whole, which is shorter than its diff:
```python
import functools
import math

import jax
import jax.numpy as jnp
from jax import lax
from jax.experimental import pallas as pl
from jax.experimental.pallas import tpu as pltpu
from jax.sharding import PartitionSpec as P

LANES = 128
MODES = 8
ROWS = 24
HIGH = lax.Precision.HIGHEST
F32 = jnp.float32

COS_TERMS = (1.0, -19.73920440673828, 64.93911743164062, -85.45014190673828, 60.167633056640625,
             -25.967601776123047, 6.528658866882324)
SIN_TERMS = (6.2831854820251465, -41.34170150756836, 81.60513305664062, -76.70301818847656,
             42.02592849731445, -14.899847984313965, 3.238137722015381)
INV_TWO_PI = 0.15915494309189535
TURN_PARTS = (6.28125, 1.93500518798828125e-3, 3.0199159819567529e-7)


def horner(terms, t):
    total = jnp.full_like(t, terms[-1])
    for term in terms[-2::-1]:
        total = total * t + F32(term)
    return total


def turn_reduce(turns):
    return turns - jnp.floor(turns + F32(0.5))


def sine(turns):
    return turns * horner(SIN_TERMS, turns * turns)


def cosine(turns):
    return horner(COS_TERMS, turns * turns)


def radians_to_turns(angle):
    whole = jnp.floor(angle * F32(INV_TWO_PI) + F32(0.5))
    rest = angle
    for part in TURN_PARTS:
        rest = rest - whole * F32(part)
    return rest * F32(INV_TWO_PI)


def powers(damping, freq, distance):
    envelope = jnp.exp(-damping * distance)
    turns = radians_to_turns(freq * distance)
    return envelope * cosine(turns), envelope * sine(turns)


def complex_mul(a, b):
    return a[0] * b[0] - a[1] * b[1], a[0] * b[1] + a[1] * b[0]


def spread(read, shape, axis):
    where = lax.broadcasted_iota(jnp.int32, shape, axis)
    total = jnp.zeros(shape, F32)
    for mode in range(MODES):
        total = jnp.where(where == mode, read(mode), total)
    return total


def tables_kernel(slabs, width, slab_ref, decay_ref, freq_ref, amp_ref, near_ref, far_ref, trans_ref, long_ref, hop_ref, coef_ref):
    shape = (MODES, LANES)
    scale = F32(1.0 / (slabs * width))
    damping = spread(lambda m: decay_ref[m], shape, 0) * scale
    freq = spread(lambda m: freq_ref[m], shape, 0)
    amps = [spread(functools.partial(lambda row, m: amp_ref[row, m], row), shape, 0) for row in range(4)]
    distance = lax.broadcasted_iota(jnp.int32, shape, 1).astype(F32)
    near = powers(damping, freq, distance)
    far = powers(damping, freq, F32(width) - distance)
    near_ref[0:8, :] = near[0]
    near_ref[8:16, :] = near[1]
    far_ref[0:8, :] = far[0]
    far_ref[8:16, :] = far[1]
    norm_trans = jnp.sqrt(2.0 * damping)
    norm_long = jnp.sqrt(damping * damping + freq * freq)
    wave_trans = jnp.sum(norm_trans * (amps[0] * near[0] - amps[1] * near[1]), axis=0, keepdims=True)
    wave_long = jnp.sum(norm_long * (amps[2] * near[0] - amps[3] * near[1]), axis=0, keepdims=True)
    square = (LANES, LANES)
    later = lax.broadcasted_iota(jnp.int32, square, 1) > lax.broadcasted_iota(jnp.int32, square, 0)
    for wave, ref in ((wave_trans, trans_ref), (wave_long, long_ref)):
        shifted = pltpu.roll(jnp.broadcast_to(wave, square), 0, 1, stride=1, stride_axis=0)
        ref[...] = jnp.where(later, shifted, F32(0.0))

    small = (slabs, MODES)
    damping = spread(lambda m: decay_ref[m], small, 1) * scale
    freq = spread(lambda m: freq_ref[m], small, 1)
    amps = [spread(functools.partial(lambda row, m: amp_ref[row, m], row), small, 1) for row in range(4)]
    norm_trans = jnp.sqrt(2.0 * damping)
    norm_long = jnp.sqrt(damping * damping + freq * freq)
    coef_ref[0] = amps[0] * norm_trans
    coef_ref[1] = amps[1] * norm_trans
    coef_ref[2] = amps[2] * norm_long
    coef_ref[3] = amps[3] * norm_long
    step = powers(damping, freq, jnp.full(small, width, F32))
    ladder = [step]
    while 2 ** len(ladder) < slabs:
        ladder.append(complex_mul(ladder[-1], ladder[-1]))
    source = lax.broadcasted_iota(jnp.int32, small, 0)
    for index in range(3):
        hops = slab_ref[0] + (index - 2) - source
        weight = (jnp.ones(small, F32), jnp.zeros(small, F32))
        for bit, factor in enumerate(ladder):
            longer = complex_mul(weight, factor)
            taken = (hops & (1 << bit)) != 0
            weight = tuple(jnp.where(taken, b, a) for a, b in zip(weight, longer))
        ahead = hops >= 0
        hop_ref[2 * index] = jnp.where(ahead, weight[0], F32(0.0))
        hop_ref[2 * index + 1] = jnp.where(ahead, weight[1], F32(0.0))


def deposit_kernel(local, capacity, fill, part_ref, index_ref, moving_ref, moment_ref, dense_ref, head_ref, tail_ref):
    tiles = local // LANES
    shape = (8, local)
    row = lax.broadcasted_iota(jnp.int32, shape, 0)
    base = jnp.where(row < 3, part_ref[0:1, :], jnp.where(row < 6, part_ref[2:3, :], F32(1.0)))
    bf = jnp.bfloat16
    high = base.astype(bf).astype(F32)
    rest = base - high
    mid = rest.astype(bf).astype(F32)
    low = rest - mid
    third = row % 3
    values = jnp.where(third == 0, high, jnp.where(third == 1, mid, low)).astype(bf)
    slot = lax.broadcasted_iota(jnp.int32, (LANES, LANES), 0)
    total = jnp.zeros((8, LANES), F32)
    group = 2
    for first in range(0, tiles, group):
        hot = jnp.concatenate(
            [(slot == index_ref[t:t + 1, :]).astype(F32).astype(bf) for t in range(first, first + group)], axis=1
        )
        total = total + lax.dot_general(
            values[:, first * LANES:(first + group) * LANES], hot, (((1,), (1,)), ((), ())), preferred_element_type=F32
        )
    root = F32(1.0 / math.sqrt(fill))
    moment_ref[0:1, :] = (total[0:1] + total[1:2] + total[2:3]) * root
    moment_ref[1:2, :] = (total[3:4] + total[4:5] + total[5:6]) * root
    moment_ref[2:3, :] = total[6:7] * F32(1.0 / fill)
    moment_ref[3:4, :] = jnp.zeros((1, LANES), F32)

    for tile in range(tiles):
        dense_ref[pl.ds(tile, 6, stride=tiles), :] = part_ref[:, tile * LANES:(tile + 1) * LANES]
    edge = capacity // LANES
    place = lax.broadcasted_iota(jnp.int32, (edge, LANES), 0) * LANES + lax.broadcasted_iota(jnp.int32, (edge, LANES), 1)
    for ref, start, leaving in (
        (head_ref, 0, place < moving_ref[0, 0, 0]),
        (tail_ref, tiles - edge, place >= capacity - moving_ref[0, 0, 1]),
    ):
        ref[0:edge, :] = jnp.zeros((edge, LANES), F32)
        for q in range(6):
            ref[edge * (q + 1):edge * (q + 2), :] = dense_ref[q * tiles + start:q * tiles + start + edge, :]
        ref[edge * 7:edge * 8, :] = jnp.where(leaving, index_ref[start:start + edge, :].astype(F32), F32(-1.0))


def pack_kernel(slabs, slab_ref, got_ref, head_ref, tail_ref, out_ref):
    moments = got_ref[0]
    for source in range(1, got_ref.shape[0]):
        moments = moments + got_ref[source]
    head, tail = head_ref[...], tail_ref[...]
    for slab in range(slabs):
        out_ref[slab] = jnp.where(slab < slab_ref[0], head, tail)
        out_ref[slab, 0:3, :] = moments[0:3]


def finish_kernel(slabs, local, capacity, slab_ref, moving_ref, got_ref, dense_ref, index_ref, near_ref, far_ref, trans_ref, long_ref,
                  hop_ref, coef_ref, kick_ref, out_ref, work_ref, done_ref):
    tiles = local // LANES
    edge = capacity // LANES
    slab = slab_ref[0]
    nt = (((1,), (1,)), ((), ()))
    moments = jnp.concatenate([got_ref[:, c, :] for c in range(3)], axis=0)
    sum_re = lax.dot_general(moments, far_ref[0:8, :], nt, precision=HIGH, preferred_element_type=F32)
    sum_im = lax.dot_general(moments, far_ref[8:16, :], nt, precision=HIGH, preferred_element_type=F32)
    line = lax.broadcasted_iota(jnp.int32, (ROWS, MODES), 0)
    carry_re = jnp.zeros((ROWS, MODES), F32)
    carry_im = jnp.zeros((ROWS, MODES), F32)
    for index in range(3):
        weight = hop_ref[2 * index], hop_ref[2 * index + 1]
        for c in range(3):
            part = complex_mul(weight, (sum_re[c * slabs:(c + 1) * slabs], sum_im[c * slabs:(c + 1) * slabs]))
            part = complex_mul(part, (coef_ref[0], coef_ref[1]) if c < 2 else (coef_ref[2], coef_ref[3]))
            here = line == 8 * index + c
            carry_re = jnp.where(here, jnp.sum(part[0], axis=0, keepdims=True), carry_re)
            carry_im = jnp.where(here, jnp.sum(part[1], axis=0, keepdims=True), carry_im)
    plain = (((1,), (0,)), ((), ()))
    incoming = lax.dot_general(carry_re, near_ref[0:8, :], plain, precision=HIGH, preferred_element_type=F32) - lax.dot_general(
        carry_im, near_ref[8:16, :], plain, precision=HIGH, preferred_element_type=F32)
    ahead = jnp.maximum(slab - 1, 0)
    behind = jnp.minimum(slab + 1, slabs - 1)
    near_moments = jnp.concatenate([got_ref[ahead, 0:8, :], got_ref[slab, 0:8, :], got_ref[behind, 0:8, :]], axis=0)
    by_trans = lax.dot_general(near_moments, trans_ref[...], plain, precision=HIGH, preferred_element_type=F32)
    by_long = lax.dot_general(near_moments, long_ref[...], plain, precision=HIGH, preferred_element_type=F32)
    wide = lax.broadcasted_iota(jnp.int32, (ROWS, LANES), 0)
    kicks = jnp.where(wide % 8 == 2, by_long, by_trans) + incoming
    kick_ref[...] = kicks[8:11]

    for q in range(6):
        work_ref[q * ROWS:q * ROWS + edge, :] = got_ref[behind, edge * (q + 1):edge * (q + 2), :]
        work_ref[q * ROWS + edge:q * ROWS + edge + tiles, :] = dense_ref[q * tiles:(q + 1) * tiles, :]
        work_ref[q * ROWS + edge + tiles:q * ROWS + 2 * edge + tiles, :] = got_ref[ahead, edge * (q + 1):edge * (q + 2), :]
        work_ref[q * ROWS + 2 * edge + tiles:(q + 1) * ROWS, :] = jnp.zeros((ROWS - 2 * edge - tiles, LANES), F32)
    base = 6 * ROWS
    own = (tiles, LANES)
    place = lax.broadcasted_iota(jnp.int32, own, 0) * LANES + lax.broadcasted_iota(jnp.int32, own, 1)
    stays = (place >= moving_ref[0, 0, 0]) & (place < local - moving_ref[0, 0, 1])
    none = F32(-1.0)
    work_ref[base:base + edge, :] = jnp.where(slab < slabs - 1, got_ref[behind, 7 * edge:8 * edge, :], none)
    work_ref[base + edge:base + edge + tiles, :] = jnp.where(stays, index_ref[...].astype(F32), none)
    work_ref[base + edge + tiles:base + 2 * edge + tiles, :] = jnp.where(slab > 0, got_ref[ahead, 7 * edge:8 * edge, :], none)
    work_ref[base + 2 * edge + tiles:base + ROWS, :] = jnp.full((ROWS - 2 * edge - tiles, LANES), -1.0, F32)

    marks = work_ref[base:base + ROWS, :]
    kept = marks >= 0.0
    index = jnp.maximum(marks, 0.0).astype(jnp.int32)

    def kick_of(c):
        table = jnp.where(wide < edge, kicks[16 + c:17 + c], jnp.where(wide < edge + tiles, kicks[8 + c:9 + c], kicks[c:c + 1]))
        return jnp.take_along_axis(table, index, axis=1)

    x, px, y, py, s, e = [work_ref[q * ROWS:(q + 1) * ROWS, :] for q in range(6)]
    px = px + kick_of(0)
    py = py + kick_of(1)
    e = e + kick_of(2)
    jx = 0.5 * (x * x + px * px)
    jy = 0.5 * (y * y + py * py)
    ux = turn_reduce(0.269 + 0.05 * e + 0.02 * e * e + 0.03 * jx - 0.02 * jy)
    uy = turn_reduce(0.355 + 0.04 * e - 0.015 * e * e + 0.03 * jy - 0.02 * jx)
    cx, sx, cy, sy = cosine(ux), sine(ux), cosine(uy), sine(uy)
    e_new = e - 0.05 * (sine(radians_to_turns(0.3 + s)) - F32(math.sin(0.3)))
    s_new = s - 0.1 * e_new
    results = (cx * x + sx * px, cx * px - sx * x, cy * y + sy * py, cy * py - sy * y, s_new, e_new)
    for q, value in enumerate(results):
        done_ref[q * ROWS:(q + 1) * ROWS, :] = jnp.where(kept, value, F32(0.0))
    for tile in range(tiles + 2 * edge):
        out_ref[:, tile * LANES:(tile + 1) * LANES] = done_ref[pl.ds(tile, 6, stride=ROWS), :]


def specs(*kinds):
    return [pl.BlockSpec(memory_space=pltpu.SMEM if kind == "s" else pltpu.VMEM) for kind in kinds]


def shape_of(*dims):
    return jax.ShapeDtypeStruct(dims, F32)


def body(particles, slice_index, moving, decay_rate, wake_freq, wake_amp):
    slabs = lax.axis_size("gz")
    members = lax.axis_size("pa")
    local = particles.shape[1]
    capacity = local * 3 // 16
    tiles = local // LANES
    fill = local * members / LANES
    slab = lax.axis_index("gz").astype(jnp.int32).reshape(1)
    index = slice_index.reshape(tiles, LANES)

    near, far, trans, long, hop, coef = pl.pallas_call(
        functools.partial(tables_kernel, slabs, LANES),
        out_shape=[shape_of(16, LANES), shape_of(16, LANES), shape_of(LANES, LANES), shape_of(LANES, LANES),
                   shape_of(6, slabs, MODES), shape_of(4, slabs, MODES)],
        in_specs=specs(*"ssss"),
        out_specs=specs(*"vvvvvv"),
        name="tables",
    )(slab, decay_rate, wake_freq, wake_amp)

    moments, dense, head, tail = pl.pallas_call(
        functools.partial(deposit_kernel, local, capacity, fill),
        out_shape=[shape_of(4, LANES), shape_of(6 * tiles, LANES), shape_of(ROWS, LANES), shape_of(ROWS, LANES)],
        in_specs=specs(*"vvs"),
        out_specs=specs(*"vvvv"),
        name="deposit",
    )(particles, index, moving)

    chips = members // 2
    pairs = [[2 * z, 2 * z + 1] for z in range(chips)]
    rings = [[2 * z + core for z in range(chips)] for core in range(2)]
    both = lax.all_gather(moments, "pa", axis_index_groups=pairs)
    spread_out = jnp.broadcast_to(both[0] + both[1], (chips, 4, LANES))
    gathered = lax.all_to_all(spread_out, "pa", 0, 0, axis_index_groups=rings)
    packed = pl.pallas_call(
        functools.partial(pack_kernel, slabs),
        out_shape=shape_of(slabs, ROWS, LANES),
        in_specs=specs(*"svvv"),
        out_specs=specs("v")[0],
        name="pack",
    )(slab, gathered, head, tail)
    everyone = lax.all_to_all(packed, "gz", 0, 0)
    return pl.pallas_call(
        functools.partial(finish_kernel, slabs, local, capacity),
        out_shape=[shape_of(3, LANES), shape_of(6, local + 2 * capacity)],
        in_specs=specs(*"ssvvvvvvvvv"),
        out_specs=specs(*"vv"),
        scratch_shapes=[pltpu.VMEM((7 * ROWS, LANES), F32), pltpu.VMEM((6 * ROWS, LANES), F32)],
        name="finish",
    )(slab, moving, everyone, dense, index, near, far, trans, long, hop, coef)


def solution(mesh):
    return jax.shard_map(
        body,
        mesh=mesh,
        in_specs=(P(None, ("gz", "pa")), P(("gz", "pa")), P("gz", "pa", None), P(), P(), P()),
        out_specs=(P(None, "gz"), P(None, ("gz", "pa"))),
        check_vma=False,
    )
```

time: 450 us -> 53.2 us (0.12)
  the two profiles are of different devices: /device:TPU:16 before, /device:TPU:2 now
where the time goes in v1:
time: 53.2 us; the launch traced here: 52.7 us
  starting transfers between devices  22.7 us (43%)
  waiting for transfers between devices  18 us (34%)
  Pallas kernels  7.03 us (13%)
  local copies, waits for them, and re-layouts  2.59 us (5%)
  blocking collectives  1.77 us (3%)
  between operations  0.65 us (1%)
    all_to_all x1, starting transfers between devices, body(): gathered = lax.all_to_all(spread_out, 'pa', 0, 0, axis_index_groups=rings)  15.2 us
    all_to_all x1, waiting for transfers between devices, body(): gathered = lax.all_to_all(spread_out, 'pa', 0, 0, axis_index_groups=rings)  12.6 us
    all_to_all x1, starting transfers between devices, body(): everyone = lax.all_to_all(packed, 'gz', 0, 0)  7.48 us
    all_to_all x1, waiting for transfers between devices, body(): everyone = lax.all_to_all(packed, 'gz', 0, 0)  5.48 us
    pallas_call x1, Pallas kernels, body(): pl.pallas_call(functools.partial(finish_kernel, slabs, local, capacity),...  2.37 us
    unnamed x6, local copies, waits for them, and re-layouts  1.96 us
    all_gather x1, blocking collectives, body(): both = lax.all_gather(moments, 'pa', axis_index_groups=pairs)  1.77 us
    pallas_call x1, Pallas kernels, body(): pl.pallas_call(functools.partial(deposit_kernel, local, capacity, fill),...  1.7 us
  transfers between devices with their start and end apart: 2, of which 2 were waited for; matrix products, arithmetic and copies ran while one was open for 0% of the time, Pallas kernels for 3%

profile of v1, /device:TPU:2, one launch (start us, length us, event | category | flops | bytes accessed | tf_op | source)
XLA Modules:
  0.0 52.7 jit_solution(12414139494780507253)
XLA Ops:
  0.6 1.7 %deposit.1 = (f32[4,128]{1,0:T(4,128)}, f32[96,128]{1,0:T(8,128)}, f32[24,128]{1,0:T(8,128)}, f32[24,128]{1,0:T(8,128)}) custom-call(f32[6,2048]{1,0:T(8,128)} %part_ref.1, s32[16,128]{1,0:T(8,128)} %bitcast.5, s32[1,1,2]{2,1,0:T(1,128)} %moving_ref.3), custom_call_target="tpu_custom_call" | custom-call | tf_op jit(solution)/shard_map/deposit/pallas_call | solution.py:272
  2.3 0.0 copy-start.2
  2.3 0.7 %copy-done.2 = f32[4,128]{1,0:T(4,128)S(1)} copy-done((f32[4,128]{1,0:T(4,128)S(1)}, f32[4,128]{1,0:T(4,128)}, u32[]{:S(2)}) %copy-start.2) | copy-done | bytes 2072
  3.0 1.8 %all-gather.1 = f32[2,4,128]{2,1,0:T(4,128)S(1)} all-gather(f32[1,4,128]{2,1,0:T(4,128)S(1)} %bitcast.7), channel_id=2, replica_groups={{0,1},{2,3},{4,5},{6,7},{8,9},{10,11},{12,13},{14,15},{16,17},{18,19},{..., dimensions={0}, use_global_device_ids=true | all-gather | bytes 6144 | tf_op jit(solution)/shard_map/all_gather | solution.py:283
  4.8 0.6 %broadcast_in_dim.3 = f32[16,4,128]{2,1,0:T(4,128)} broadcast(f32[4,128]{1,0:T(4,128)S(1)} %fusion), dimensions={1,2} | broadcast | bytes 34816 | tf_op jit(solution)/shard_map/broadcast_in_dim | solution.py:284
  5.4 15.2 %all-to-all-start = ((f32[16,4,128]{2,1,0:T(4,128)}), f32[16,4,128]{2,1,0:T(4,128)S(1)}, u32[]{:S(2)}, u32[]{:S(2)}) async-start(f32[16,4,128]{2,1,0:T(4,128)} %broadcast_in_dim.3), calls=%async_computation | async-start | bytes 65536 | tf_op jit(solution)/shard_map/all_to_all | solution.py:285
  20.6 12.6 %all-to-all-done.got_ref = f32[16,4,128]{2,1,0:T(4,128)S(1)} async-done(((f32[16,4,128]{2,1,0:T(4,128)}), f32[16,4,128]{2,1,0:T(4,128)S(1)}, u32[]{:S(2)}, u32[]{:S(2)}) %all-to-all-start) | async-done | bytes 32800 | tf_op jit(solution)/shard_map/all_to_all | solution.py:285
  33.2 0.0 copy-start.1
  33.2 0.6 %copy-done.1 = f32[16,4,128]{2,1,0:T(4,128)} copy-done((f32[16,4,128]{2,1,0:T(4,128)}, f32[16,4,128]{2,1,0:T(4,128)S(1)}, u32[]{:S(2)}) %copy-start.1) | copy-done | bytes 32792
  33.8 1.5 %pack.1 = f32[16,24,128]{2,1,0:T(8,128)} custom-call(s32[1]{0:T(128)} %bitcast.slab_ref, f32[16,4,128]{2,1,0:T(4,128)} %copy-done.1, f32[24,128]{1,0:T(8,128)} %get-tuple-element.13.head_ref, f32[24,128]{1,0:T(8,128)} %get-tuple-element.14.tail_ref), custom_call_target="tpu_custom_call" | custom-call | tf_op jit(solution)/shard_map/pack/pallas_call | solution.py:286
  35.2 7.5 %all-to-all-start.1 = ((f32[16,24,128]{2,1,0:T(8,128)}), f32[16,24,128]{2,1,0:T(8,128)S(1)}, u32[]{:S(2)}, u32[]{:S(2)}) async-start(f32[16,24,128]{2,1,0:T(8,128)} %pack.1), calls=%async_computation.1 | async-start | bytes 393216 | tf_op jit(solution)/shard_map/all_to_all | solution.py:293
  42.7 1.5 %tables.1 = (f32[16,128]{1,0:T(8,128)}, f32[16,128]{1,0:T(8,128)}, f32[128,128]{1,0:T(8,128)}, f32[128,128]{1,0:T(8,128)}, f32[6,16,8]{2,1,0:T(8,128)}, /*index=5*/f32[4,16,8]{2,1,0:T(8,128)}) custom-call(s32[1]{0:T(128)} %bitcast.slab_ref, f32[8]{0:T(128)} %decay_ref.1, f32[8]{0:T(128)} %freq_ref.1, f32[4,8]{1,0:T(4,128)} %amp_ref.1), custom_call_target="tpu_custom_call" | custom-call | tf_op jit(solution)/shard_map/tables/pallas_call | solution.py:263
  44.2 5.5 %all-to-all-done.1.got_ref = f32[16,24,128]{2,1,0:T(8,128)S(1)} async-done(((f32[16,24,128]{2,1,0:T(8,128)}), f32[16,24,128]{2,1,0:T(8,128)S(1)}, u32[]{:S(2)}, u32[]{:S(2)}) %all-to-all-start.1) | async-done | bytes 196640 | tf_op jit(solution)/shard_map/all_to_all | solution.py:293
  49.7 0.0 copy-start
  49.7 0.7 %copy-done = f32[16,24,128]{2,1,0:T(8,128)} copy-done((f32[16,24,128]{2,1,0:T(8,128)}, f32[16,24,128]{2,1,0:T(8,128)S(1)}, u32[]{:S(2)}) %copy-start) | copy-done | bytes 196632
  50.4 2.4 %finish.1 = (f32[3,128]{1,0:T(4,128)}, f32[6,2816]{1,0:T(8,128)}) custom-call(s32[1]{0:T(128)} %bitcast.slab_ref, s32[1,1,2]{2,1,0:T(1,128)} %moving_ref.3, f32[16,24,128]{2,1,0:T(8,128)} %copy-done, f32[96,128]{1,0:T(8,128)} %get-tuple-element.15.dense_ref, s32[16,128]{1,0:T(8,128)} %bitcast.6, f32[16,128]{1,0:T(8,128)} %get-tuple-element.16.near_ref, ...), custom_call_target="tpu_custom_call" | custom-call | tf_op jit(solution)/shard_map/finish/pallas_call | solution.py:294
  (1 shorter events, 0.0 us)
Async XLA Ops:
  2.3 0.7 %copy-start.2 = (f32[4,128]{1,0:T(4,128)S(1)}, f32[4,128]{1,0:T(4,128)}, u32[]{:S(2)}) copy-start(f32[4,128]{1,0:T(4,128)} %get-tuple-element.12) | copy-start | bytes 6148
  5.4 27.8 %all-to-all-start = ((f32[16,4,128]{2,1,0:T(4,128)}), f32[16,4,128]{2,1,0:T(4,128)S(1)}, u32[]{:S(2)}, u32[]{:S(2)}) async-start(f32[16,4,128]{2,1,0:T(4,128)} %broadcast_in_dim.3), calls=%async_computation | async-start | bytes 65536 | tf_op jit(solution)/shard_map/all_to_all | solution.py:285
  33.2 0.6 %copy-start.1 = (f32[16,4,128]{2,1,0:T(4,128)}, f32[16,4,128]{2,1,0:T(4,128)S(1)}, u32[]{:S(2)}) copy-start(f32[16,4,128]{2,1,0:T(4,128)S(1)} %all-to-all-done.got_ref) | copy-start | bytes 98308
  35.2 14.5 %all-to-all-start.1 = ((f32[16,24,128]{2,1,0:T(8,128)}), f32[16,24,128]{2,1,0:T(8,128)S(1)}, u32[]{:S(2)}, u32[]{:S(2)}) async-start(f32[16,24,128]{2,1,0:T(8,128)} %pack.1), calls=%async_computation.1 | async-start | bytes 393216 | tf_op jit(solution)/shard_map/all_to_all | solution.py:293
  49.7 0.7 %copy-start = (f32[16,24,128]{2,1,0:T(8,128)}, f32[16,24,128]{2,1,0:T(8,128)S(1)}, u32[]{:S(2)}) copy-start(f32[16,24,128]{2,1,0:T(8,128)S(1)} %all-to-all-done.1.got_ref) | copy-start | bytes 589828

commit v2 on v1

--- a/solution.py
+++ b/solution.py
@@ -18,6 +18,9 @@
              -25.967601776123047, 6.528658866882324)
 SIN_TERMS = (6.2831854820251465, -41.34170150756836, 81.60513305664062, -76.70301818847656,
              42.02592849731445, -14.899847984313965, 3.238137722015381)
+SMALL = pltpu.CompilerParams(vmem_limit_bytes=4 << 20)
+FIRST_RING = 8
+FIRST_SLAB = 10
 INV_TWO_PI = 0.15915494309189535
 TURN_PARTS = (6.28125, 1.93500518798828125e-3, 3.0199159819567529e-7)
 
@@ -67,7 +70,7 @@
     return total
 
 
-def tables_kernel(slabs, width, slab_ref, decay_ref, freq_ref, amp_ref, near_ref, far_ref, trans_ref, long_ref, hop_ref, coef_ref):
+def make_tables(slabs, width, slab_ref, decay_ref, freq_ref, amp_ref, near_ref, far_ref, trans_ref, long_ref, hop_ref, coef_ref):
     shape = (MODES, LANES)
     scale = F32(1.0 / (slabs * width))
     damping = spread(lambda m: decay_ref[m], shape, 0) * scale
@@ -104,7 +107,7 @@
     ladder = [step]
     while 2 ** len(ladder) < slabs:
         ladder.append(complex_mul(ladder[-1], ladder[-1]))
-    source = lax.broadcasted_iota(jnp.int32, small, 0)
+    source = lax.broadcasted_iota(jnp.int32, small, 0) ^ FIRST_SLAB
     for index in range(3):
         hops = slab_ref[0] + (index - 2) - source
         weight = (jnp.ones(small, F32), jnp.zeros(small, F32))
@@ -117,8 +120,17 @@
         hop_ref[2 * index + 1] = jnp.where(ahead, weight[1], F32(0.0))
 
 
-def deposit_kernel(local, capacity, fill, part_ref, index_ref, moving_ref, moment_ref, dense_ref, head_ref, tail_ref):
+def fetch(sources, targets, sems):
+    copies = [pltpu.make_async_copy(a, b, sems.at[k]) for k, (a, b) in enumerate(zip(sources, targets))]
+    for copy in copies:
+        copy.start()
+    for copy in copies:
+        copy.wait()
+
+
+def deposit_kernel(local, fill, part_hbm, index_hbm, moment_ref, part_ref, index_ref, sems):
     tiles = local // LANES
+    fetch((part_hbm, index_hbm), (part_ref, index_ref), sems)
     shape = (8, local)
     row = lax.broadcasted_iota(jnp.int32, shape, 0)
     base = jnp.where(row < 3, part_ref[0:1, :], jnp.where(row < 6, part_ref[2:3, :], F32(1.0)))
@@ -145,6 +157,9 @@
     moment_ref[2:3, :] = total[6:7] * F32(1.0 / fill)
     moment_ref[3:4, :] = jnp.zeros((1, LANES), F32)
 
+
+def make_payload(local, capacity, part_ref, index_ref, moving_ref, dense_ref, head_ref, tail_ref):
+    tiles = local // LANES
     for tile in range(tiles):
         dense_ref[pl.ds(tile, 6, stride=tiles), :] = part_ref[:, tile * LANES:(tile + 1) * LANES]
     edge = capacity // LANES
@@ -159,14 +174,28 @@
         ref[edge * 7:edge * 8, :] = jnp.where(leaving, index_ref[start:start + edge, :].astype(F32), F32(-1.0))
 
 
+def prepare_kernel(slabs, local, capacity, slab_ref, part_hbm, index_hbm, moving_hbm, decay_hbm, freq_hbm, amp_hbm, *refs):
+    outs, (part_ref, index_ref, moving_ref, decay_ref, freq_ref, amp_ref, sems) = refs[:9], refs[9:]
+    fetch((part_hbm, index_hbm, moving_hbm, decay_hbm, freq_hbm, amp_hbm),
+          (part_ref, index_ref, moving_ref, decay_ref, freq_ref, amp_ref), sems)
+    make_payload(local, capacity, part_ref, index_ref, moving_ref, *outs[:3])
+    make_tables(slabs, LANES, slab_ref, decay_ref, freq_ref, amp_ref, *outs[3:])
+
+
+def repeat_kernel(both_ref, out_ref):
+    total = both_ref[0] + both_ref[1]
+    for slot in range(out_ref.shape[0]):
+        out_ref[slot] = total
+
+
 def pack_kernel(slabs, slab_ref, got_ref, head_ref, tail_ref, out_ref):
     moments = got_ref[0]
     for source in range(1, got_ref.shape[0]):
         moments = moments + got_ref[source]
     head, tail = head_ref[...], tail_ref[...]
-    for slab in range(slabs):
-        out_ref[slab] = jnp.where(slab < slab_ref[0], head, tail)
-        out_ref[slab, 0:3, :] = moments[0:3]
+    for slot in range(slabs):
+        out_ref[slot] = jnp.where((slot ^ FIRST_SLAB) < slab_ref[0], head, tail)
+        out_ref[slot, 0:3, :] = moments[0:3]
 
 
 def finish_kernel(slabs, local, capacity, slab_ref, moving_ref, got_ref, dense_ref, index_ref, near_ref, far_ref, trans_ref, long_ref,
@@ -192,9 +221,9 @@
     plain = (((1,), (0,)), ((), ()))
     incoming = lax.dot_general(carry_re, near_ref[0:8, :], plain, precision=HIGH, preferred_element_type=F32) - lax.dot_general(
         carry_im, near_ref[8:16, :], plain, precision=HIGH, preferred_element_type=F32)
-    ahead = jnp.maximum(slab - 1, 0)
-    behind = jnp.minimum(slab + 1, slabs - 1)
-    near_moments = jnp.concatenate([got_ref[ahead, 0:8, :], got_ref[slab, 0:8, :], got_ref[behind, 0:8, :]], axis=0)
+    ahead = jnp.maximum(slab - 1, 0) ^ FIRST_SLAB
+    behind = jnp.minimum(slab + 1, slabs - 1) ^ FIRST_SLAB
+    near_moments = jnp.concatenate([got_ref[ahead, 0:8, :], got_ref[slab ^ FIRST_SLAB, 0:8, :], got_ref[behind, 0:8, :]], axis=0)
     by_trans = lax.dot_general(near_moments, trans_ref[...], plain, precision=HIGH, preferred_element_type=F32)
     by_long = lax.dot_general(near_moments, long_ref[...], plain, precision=HIGH, preferred_element_type=F32)
     wide = lax.broadcasted_iota(jnp.int32, (ROWS, LANES), 0)
@@ -243,7 +272,11 @@
 
 
 def specs(*kinds):
-    return [pl.BlockSpec(memory_space=pltpu.SMEM if kind == "s" else pltpu.VMEM) for kind in kinds]
+    return [pl.BlockSpec(memory_space={"s": pltpu.SMEM, "v": pltpu.VMEM, "h": pltpu.HBM}[kind]) for kind in kinds]
+
+
+def stay(array):
+    return pltpu.with_memory_space_constraint(array, pltpu.HBM)
 
 
 def shape_of(*dims):
@@ -260,43 +293,62 @@
     slab = lax.axis_index("gz").astype(jnp.int32).reshape(1)
     index = slice_index.reshape(tiles, LANES)
 
-    near, far, trans, long, hop, coef = pl.pallas_call(
-        functools.partial(tables_kernel, slabs, LANES),
-        out_shape=[shape_of(16, LANES), shape_of(16, LANES), shape_of(LANES, LANES), shape_of(LANES, LANES),
+    moments = pl.pallas_call(
+        functools.partial(deposit_kernel, local, fill),
+        out_shape=shape_of(4, LANES),
+        in_specs=specs(*"hh"),
+        out_specs=specs("v")[0],
+        scratch_shapes=[pltpu.VMEM((6, local), F32), pltpu.VMEM((tiles, LANES), jnp.int32), pltpu.SemaphoreType.DMA((2,))],
+        compiler_params=SMALL,
+        name="deposit",
+    )(stay(particles), stay(index))
+    dense, head, tail, near, far, trans, long, hop, coef = pl.pallas_call(
+        functools.partial(prepare_kernel, slabs, local, capacity),
+        out_shape=[shape_of(6 * tiles, LANES), shape_of(ROWS, LANES), shape_of(ROWS, LANES),
+                   shape_of(16, LANES), shape_of(16, LANES), shape_of(LANES, LANES), shape_of(LANES, LANES),
                    shape_of(6, slabs, MODES), shape_of(4, slabs, MODES)],
-        in_specs=specs(*"ssss"),
-        out_specs=specs(*"vvvvvv"),
-        name="tables",
-    )(slab, decay_rate, wake_freq, wake_amp)
-
-    moments, dense, head, tail = pl.pallas_call(
-        functools.partial(deposit_kernel, local, capacity, fill),
-        out_shape=[shape_of(4, LANES), shape_of(6 * tiles, LANES), shape_of(ROWS, LANES), shape_of(ROWS, LANES)],
-        in_specs=specs(*"vvs"),
-        out_specs=specs(*"vvvv"),
-        name="deposit",
-    )(particles, index, moving)
+        in_specs=specs(*"shhhhhh"),
+        out_specs=specs(*"vvvvvvvvv"),
+        scratch_shapes=[pltpu.VMEM((6, local), F32), pltpu.VMEM((tiles, LANES), jnp.int32), pltpu.SMEM((1, 1, 2), jnp.int32),
+                        pltpu.SMEM((MODES,), F32), pltpu.SMEM((MODES,), F32), pltpu.SMEM((4, MODES), F32),
+                        pltpu.SemaphoreType.DMA((6,))],
+        compiler_params=SMALL,
+        name="prepare",
+    )(slab, *[stay(array) for array in (particles, index, moving, decay_rate, wake_freq, wake_amp)])
 
     chips = members // 2
-    pairs = [[2 * z, 2 * z + 1] for z in range(chips)]
-    rings = [[2 * z + core for z in range(chips)] for core in range(2)]
+    pairs = [[2 * z + 1, 2 * z] for z in range(chips)]
+    rings = [[2 * ((z + FIRST_RING) % chips) + core for z in range(chips)] for core in range(2)]
+    order = [slot ^ FIRST_SLAB for slot in range(slabs)]
     both = lax.all_gather(moments, "pa", axis_index_groups=pairs)
-    spread_out = jnp.broadcast_to(both[0] + both[1], (chips, 4, LANES))
-    gathered = lax.all_to_all(spread_out, "pa", 0, 0, axis_index_groups=rings)
+    repeated = pl.pallas_call(
+        repeat_kernel,
+        out_shape=pltpu.VMEM((chips, 4, LANES), F32),
+        in_specs=specs("v"),
+        out_specs=specs("v")[0],
+        compiler_params=SMALL,
+        name="repeat",
+    )(both)
+    gathered = lax.all_to_all(repeated, "pa", 0, 0, axis_index_groups=rings)
+    gathered, dense, head, tail, near, far, trans, long, hop, coef = lax.optimization_barrier(
+        (gathered, dense, head, tail, near, far, trans, long, hop, coef)
+    )
     packed = pl.pallas_call(
         functools.partial(pack_kernel, slabs),
-        out_shape=shape_of(slabs, ROWS, LANES),
+        out_shape=pltpu.VMEM((slabs, ROWS, LANES), F32),
         in_specs=specs(*"svvv"),
         out_specs=specs("v")[0],
+        compiler_params=SMALL,
         name="pack",
     )(slab, gathered, head, tail)
-    everyone = lax.all_to_all(packed, "gz", 0, 0)
+    everyone = lax.all_to_all(packed, "gz", 0, 0, axis_index_groups=[order])
     return pl.pallas_call(
         functools.partial(finish_kernel, slabs, local, capacity),
         out_shape=[shape_of(3, LANES), shape_of(6, local + 2 * capacity)],
         in_specs=specs(*"ssvvvvvvvvv"),
         out_specs=specs(*"vv"),
         scratch_shapes=[pltpu.VMEM((7 * ROWS, LANES), F32), pltpu.VMEM((6 * ROWS, LANES), F32)],
+        compiler_params=SMALL,
         name="finish",
     )(slab, moving, everyone, dense, index, near, far, trans, long, hop, coef)
 

time: 53.2 us -> 40.2 us (0.76)
  the two profiles are of different devices: /device:TPU:2 before, /device:TPU:4 now
where the time goes in v2:
time: 40.2 us; the launch traced here: 39.9 us
  starting transfers between devices  18.9 us (47%)
  blocking collectives  13.7 us (34%)
  Pallas kernels  4.66 us (12%)
  waiting for transfers between devices  1.93 us (5%)
  between operations  0.67 us (2%)
    all_to_all x1, starting transfers between devices, body(): gathered = lax.all_to_all(repeated, 'pa', 0, 0, axis_index_groups=rings)  18.9 us
    all_to_all x1, blocking collectives, body(): everyone = lax.all_to_all(packed, 'gz', 0, 0, axis_index_groups=[order])  12 us
    all_to_all x1, waiting for transfers between devices, body(): gathered = lax.all_to_all(repeated, 'pa', 0, 0, axis_index_groups=rings)  1.93 us
    pallas_call x1, Pallas kernels, body(): pl.pallas_call(functools.partial(finish_kernel, slabs, local, capacity),...  1.83 us
    all_gather x1, blocking collectives, body(): both = lax.all_gather(moments, 'pa', axis_index_groups=pairs)  1.78 us
    pallas_call x1, Pallas kernels, body(): pl.pallas_call(functools.partial(deposit_kernel, local, fill), out_shape=...  1.12 us
    pallas_call x1, Pallas kernels, body(): pl.pallas_call(functools.partial(prepare_kernel, slabs, local, capacity),...  1.07 us
  transfers between devices with their start and end apart: 1, of which 1 were waited for; matrix products, arithmetic and copies ran while one was open for 0% of the time, Pallas kernels for 3%

profile of v2, /device:TPU:4, one launch (start us, length us, event | category | flops | bytes accessed | tf_op | source)
XLA Modules:
  0.0 39.9 jit_solution(145367925012549258)
XLA Ops:
  0.6 1.1 %deposit.1 = f32[4,128]{1,0:T(4,128)S(1)} custom-call(f32[6,2048]{1,0:T(8,128)} %part_hbm.3, s32[16,128]{1,0:T(8,128)} %bitcast.3), custom_call_target="tpu_custom_call" | custom-call | tf_op jit(solution)/shard_map/deposit/pallas_call | solution.py:296
  1.8 1.8 %all-gather.1.both_ref = f32[2,4,128]{2,1,0:T(4,128)S(1)} all-gather(f32[1,4,128]{2,1,0:T(4,128)S(1)} %bitcast.6), channel_id=2, replica_groups={{1,0},{3,2},{5,4},{7,6},{9,8},{11,10},{13,12},{15,14},{17,16},{19,18},{..., dimensions={0}, use_global_device_ids=true | all-gather | bytes 6144 | tf_op jit(solution)/shard_map/all_gather | solution.py:323
  3.5 0.6 %repeat.1 = f32[16,4,128]{2,1,0:T(4,128)} custom-call(f32[2,4,128]{2,1,0:T(4,128)S(1)} %all-gather.1.both_ref), custom_call_target="tpu_custom_call" | custom-call | tf_op jit(solution)/shard_map/repeat/pallas_call | solution.py:324
  4.2 18.9 %all-to-all-start = ((f32[16,4,128]{2,1,0:T(4,128)}), f32[16,4,128]{2,1,0:T(4,128)S(1)}, u32[]{:S(2)}, u32[]{:S(2)}) async-start(f32[16,4,128]{2,1,0:T(4,128)} %repeat.1), calls=%async_computation | async-start | bytes 65536 | tf_op jit(solution)/shard_map/all_to_all | solution.py:332
  23.0 1.1 %prepare.1 = (f32[96,128]{1,0:T(8,128)S(1)}, f32[24,128]{1,0:T(8,128)S(1)}, f32[24,128]{1,0:T(8,128)S(1)}, f32[16,128]{1,0:T(8,128)S(1)}, f32[16,128]{1,0:T(8,12...) custom-call(s32[1]{0:T(128)} %bitcast.slab_ref, ...), custom_call_target="tpu_custom_call" | custom-call | tf_op jit(solution)/shard_map/prepare/pallas_call | solution.py:305
  24.1 1.9 %all-to-all-done.got_ref = f32[16,4,128]{2,1,0:T(4,128)S(1)} async-done(((f32[16,4,128]{2,1,0:T(4,128)}), f32[16,4,128]{2,1,0:T(4,128)S(1)}, u32[]{:S(2)}, u32[]{:S(2)}) %all-to-all-start) | async-done | bytes 32800 | tf_op jit(solution)/shard_map/all_to_all | solution.py:332
  26.0 0.0 copy-start
  26.1 0.0 copy-start.1
  26.1 12.0 %all_to_all.10.got_ref = f32[16,24,128]{2,1,0:T(8,128)S(1)} all-to-all(f32[16,24,128]{2,1,0:T(8,128)S(1)} %pack.1), channel_id=1, replica_groups={{320,352,256,288,448,480,384,416,64,96,0,32,192,224,128,160},{321,353,2..., dimensions={0} | all-to-all | bytes 393216 | tf_op jit(solution)/shard_map/all_to_all | solution.py:344
  38.0 0.0 copy-done
  38.0 0.0 copy-done.1
  38.0 1.8 %finish.1 = (f32[3,128]{1,0:T(4,128)}, f32[6,2816]{1,0:T(8,128)}) custom-call(s32[1]{0:T(128)} %bitcast.slab_ref, s32[1,1,2]{2,1,0:T(1,128)S(1)} %copy-done.1, f32[16,24,128]{2,1,0:T(8,128)S(1)} %all_to_all.10.got_ref, f32[96,128]{1,0:T(8,128)S(1)} %get-tuple-element.33.dense_ref, s32[16,128]{1,0:T(8,128)S(1)} %bitcast.5, ...), custom_call_target="tpu_custom_call" | custom-call | tf_op jit(solution)/shard_map/finish/pallas_call | solution.py:345
  (1 shorter events, 0.0 us)
Async XLA Ops:
  4.2 21.9 %all-to-all-start = ((f32[16,4,128]{2,1,0:T(4,128)}), f32[16,4,128]{2,1,0:T(4,128)S(1)}, u32[]{:S(2)}, u32[]{:S(2)}) async-start(f32[16,4,128]{2,1,0:T(4,128)} %repeat.1), calls=%async_computation | async-start | bytes 65536 | tf_op jit(solution)/shard_map/all_to_all | solution.py:332
  26.0 12.0 %copy-start = (s32[2048]{0:T(1024)S(1)}, s32[2048]{0:T(1024)}, u32[]{:S(2)}) copy-start(s32[2048]{0:T(1024)} %param.7) | copy-start | bytes 24580
  26.1 12.0 %copy-start.1 = (s32[1,1,2]{2,1,0:T(1,128)S(1)}, s32[1,1,2]{2,1,0:T(1,128)}, u32[]{:S(2)}) copy-start(s32[1,1,2]{2,1,0:T(1,128)} %moving_ref.1) | copy-start | bytes 28

commit v3 on v2

--- a/solution.py
+++ b/solution.py
@@ -128,9 +128,8 @@
         copy.wait()
 
 
-def deposit_kernel(local, fill, part_hbm, index_hbm, moment_ref, part_ref, index_ref, sems):
+def deposit(local, fill, part_ref, index_ref, moment_ref):
     tiles = local // LANES
-    fetch((part_hbm, index_hbm), (part_ref, index_ref), sems)
     shape = (8, local)
     row = lax.broadcasted_iota(jnp.int32, shape, 0)
     base = jnp.where(row < 3, part_ref[0:1, :], jnp.where(row < 6, part_ref[2:3, :], F32(1.0)))
@@ -162,6 +161,10 @@
     tiles = local // LANES
     for tile in range(tiles):
         dense_ref[pl.ds(tile, 6, stride=tiles), :] = part_ref[:, tile * LANES:(tile + 1) * LANES]
+    own = (tiles, LANES)
+    position = lax.broadcasted_iota(jnp.int32, own, 0) * LANES + lax.broadcasted_iota(jnp.int32, own, 1)
+    stays = (position >= moving_ref[0, 0, 0]) & (position < local - moving_ref[0, 0, 1])
+    dense_ref[6 * tiles:7 * tiles, :] = jnp.where(stays, index_ref[...].astype(F32), F32(-1.0))
     edge = capacity // LANES
     place = lax.broadcasted_iota(jnp.int32, (edge, LANES), 0) * LANES + lax.broadcasted_iota(jnp.int32, (edge, LANES), 1)
     for ref, start, leaving in (
@@ -174,12 +177,13 @@
         ref[edge * 7:edge * 8, :] = jnp.where(leaving, index_ref[start:start + edge, :].astype(F32), F32(-1.0))
 
 
-def prepare_kernel(slabs, local, capacity, slab_ref, part_hbm, index_hbm, moving_hbm, decay_hbm, freq_hbm, amp_hbm, *refs):
-    outs, (part_ref, index_ref, moving_ref, decay_ref, freq_ref, amp_ref, sems) = refs[:9], refs[9:]
+def deposit_kernel(slabs, local, capacity, fill, slab_ref, part_hbm, index_hbm, moving_hbm, decay_hbm, freq_hbm, amp_hbm, *refs):
+    outs, (part_ref, index_ref, moving_ref, decay_ref, freq_ref, amp_ref, sems) = refs[:10], refs[10:]
     fetch((part_hbm, index_hbm, moving_hbm, decay_hbm, freq_hbm, amp_hbm),
           (part_ref, index_ref, moving_ref, decay_ref, freq_ref, amp_ref), sems)
-    make_payload(local, capacity, part_ref, index_ref, moving_ref, *outs[:3])
-    make_tables(slabs, LANES, slab_ref, decay_ref, freq_ref, amp_ref, *outs[3:])
+    deposit(local, fill, part_ref, index_ref, outs[0])
+    make_payload(local, capacity, part_ref, index_ref, moving_ref, *outs[1:4])
+    make_tables(slabs, LANES, slab_ref, decay_ref, freq_ref, amp_ref, *outs[4:])
 
 
 def repeat_kernel(both_ref, out_ref):
@@ -198,7 +202,7 @@
         out_ref[slot, 0:3, :] = moments[0:3]
 
 
-def finish_kernel(slabs, local, capacity, slab_ref, moving_ref, got_ref, dense_ref, index_ref, near_ref, far_ref, trans_ref, long_ref,
+def finish_kernel(slabs, local, capacity, slab_ref, got_ref, dense_ref, near_ref, far_ref, trans_ref, long_ref,
                   hop_ref, coef_ref, kick_ref, out_ref, work_ref, done_ref):
     tiles = local // LANES
     edge = capacity // LANES
@@ -236,12 +240,9 @@
         work_ref[q * ROWS + edge + tiles:q * ROWS + 2 * edge + tiles, :] = got_ref[ahead, edge * (q + 1):edge * (q + 2), :]
         work_ref[q * ROWS + 2 * edge + tiles:(q + 1) * ROWS, :] = jnp.zeros((ROWS - 2 * edge - tiles, LANES), F32)
     base = 6 * ROWS
-    own = (tiles, LANES)
-    place = lax.broadcasted_iota(jnp.int32, own, 0) * LANES + lax.broadcasted_iota(jnp.int32, own, 1)
-    stays = (place >= moving_ref[0, 0, 0]) & (place < local - moving_ref[0, 0, 1])
     none = F32(-1.0)
     work_ref[base:base + edge, :] = jnp.where(slab < slabs - 1, got_ref[behind, 7 * edge:8 * edge, :], none)
-    work_ref[base + edge:base + edge + tiles, :] = jnp.where(stays, index_ref[...].astype(F32), none)
+    work_ref[base + edge:base + edge + tiles, :] = dense_ref[6 * tiles:7 * tiles, :]
     work_ref[base + edge + tiles:base + 2 * edge + tiles, :] = jnp.where(slab > 0, got_ref[ahead, 7 * edge:8 * edge, :], none)
     work_ref[base + 2 * edge + tiles:base + ROWS, :] = jnp.full((ROWS - 2 * edge - tiles, LANES), -1.0, F32)
 
@@ -293,27 +294,18 @@
     slab = lax.axis_index("gz").astype(jnp.int32).reshape(1)
     index = slice_index.reshape(tiles, LANES)
 
-    moments = pl.pallas_call(
-        functools.partial(deposit_kernel, local, fill),
-        out_shape=shape_of(4, LANES),
-        in_specs=specs(*"hh"),
-        out_specs=specs("v")[0],
-        scratch_shapes=[pltpu.VMEM((6, local), F32), pltpu.VMEM((tiles, LANES), jnp.int32), pltpu.SemaphoreType.DMA((2,))],
-        compiler_params=SMALL,
-        name="deposit",
-    )(stay(particles), stay(index))
-    dense, head, tail, near, far, trans, long, hop, coef = pl.pallas_call(
-        functools.partial(prepare_kernel, slabs, local, capacity),
-        out_shape=[shape_of(6 * tiles, LANES), shape_of(ROWS, LANES), shape_of(ROWS, LANES),
+    moments, dense, head, tail, near, far, trans, long, hop, coef = pl.pallas_call(
+        functools.partial(deposit_kernel, slabs, local, capacity, fill),
+        out_shape=[shape_of(4, LANES), shape_of(7 * tiles, LANES), shape_of(ROWS, LANES), shape_of(ROWS, LANES),
                    shape_of(16, LANES), shape_of(16, LANES), shape_of(LANES, LANES), shape_of(LANES, LANES),
                    shape_of(6, slabs, MODES), shape_of(4, slabs, MODES)],
         in_specs=specs(*"shhhhhh"),
-        out_specs=specs(*"vvvvvvvvv"),
+        out_specs=specs(*"vvvvvvvvvv"),
         scratch_shapes=[pltpu.VMEM((6, local), F32), pltpu.VMEM((tiles, LANES), jnp.int32), pltpu.SMEM((1, 1, 2), jnp.int32),
                         pltpu.SMEM((MODES,), F32), pltpu.SMEM((MODES,), F32), pltpu.SMEM((4, MODES), F32),
                         pltpu.SemaphoreType.DMA((6,))],
         compiler_params=SMALL,
-        name="prepare",
+        name="deposit",
     )(slab, *[stay(array) for array in (particles, index, moving, decay_rate, wake_freq, wake_amp)])
 
     chips = members // 2
@@ -330,9 +322,6 @@
         name="repeat",
     )(both)
     gathered = lax.all_to_all(repeated, "pa", 0, 0, axis_index_groups=rings)
-    gathered, dense, head, tail, near, far, trans, long, hop, coef = lax.optimization_barrier(
-        (gathered, dense, head, tail, near, far, trans, long, hop, coef)
-    )
     packed = pl.pallas_call(
         functools.partial(pack_kernel, slabs),
         out_shape=pltpu.VMEM((slabs, ROWS, LANES), F32),
@@ -345,12 +334,12 @@
     return pl.pallas_call(
         functools.partial(finish_kernel, slabs, local, capacity),
         out_shape=[shape_of(3, LANES), shape_of(6, local + 2 * capacity)],
-        in_specs=specs(*"ssvvvvvvvvv"),
+        in_specs=specs(*"svvvvvvvv"),
         out_specs=specs(*"vv"),
         scratch_shapes=[pltpu.VMEM((7 * ROWS, LANES), F32), pltpu.VMEM((6 * ROWS, LANES), F32)],
         compiler_params=SMALL,
         name="finish",
-    )(slab, moving, everyone, dense, index, near, far, trans, long, hop, coef)
+    )(slab, everyone, dense, near, far, trans, long, hop, coef)
 
 
 def solution(mesh):

time: 40.2 us -> 38.8 us (0.965)
  blocking collectives: 13.7 us -> 35.4 us
  starting transfers between devices: 18.9 us -> 0 us
  Pallas kernels: 4.66 us -> 2.58 us
  waiting for transfers between devices: 1.93 us -> 0 us
    all_to_all x0 -> x1, blocking collectives: none -> 21.7 us  [body(): gathered = lax.all_to_all(repeated, 'pa', 0, 0, axis_index_groups=rings)]
    all_to_all x1 -> x0, starting transfers between devices: 18.9 us -> none  [body(): gathered = lax.all_to_all(repeated, 'pa', 0, 0, axis_index_groups=rings)]
    all_to_all x1 -> x0, waiting for transfers between devices: 1.93 us -> none  [body(): gathered = lax.all_to_all(repeated, 'pa', 0, 0, axis_index_groups=rings)]
    pallas_call x2 -> x1, Pallas kernels: 2.19 us -> 1.27 us  [body(): pl.pallas_call(functools.partial(deposit_kernel, slabs, local, capacity,...]
    pallas_call x1, Pallas kernels: 0.62 us -> 0.01 us  [body(): pl.pallas_call(repeat_kernel, out_shape=pltpu.VMEM((chips, 4, LANES), F32...]
    pallas_call x1, Pallas kernels: 1.83 us -> 1.28 us  [body(): pl.pallas_call(functools.partial(finish_kernel, slabs, local, capacity),...]
  transfers between devices with their start and end apart: 1 -> 0, of which waited for: 1 -> 0; matrix products, arithmetic and copies ran while one was open for 0% -> 0% of each run, Pallas kernels for 3% -> 0%
where the time goes in v3:
time: 38.8 us; the launch traced here: 38.6 us
  blocking collectives  35.4 us (91%)
  Pallas kernels  2.58 us (7%)
  between operations  0.65 us (2%)
    all_to_all x1, blocking collectives, body(): gathered = lax.all_to_all(repeated, 'pa', 0, 0, axis_index_groups=rings)  21.7 us
    all_to_all x1, blocking collectives, body(): everyone = lax.all_to_all(packed, 'gz', 0, 0, axis_index_groups=[order])  12 us
    all_gather x1, blocking collectives, body(): both = lax.all_gather(moments, 'pa', axis_index_groups=pairs)  1.78 us
    pallas_call x1, Pallas kernels, body(): pl.pallas_call(functools.partial(finish_kernel, slabs, local, capacity),...  1.28 us
    pallas_call x1, Pallas kernels, body(): pl.pallas_call(functools.partial(deposit_kernel, slabs, local, capacity,...  1.27 us

profile of v3, /device:TPU:4, one launch (start us, length us, event | category | flops | bytes accessed | tf_op | source)
XLA Modules:
  0.0 38.6 jit_solution(10917540172335863883)
XLA Ops:
  0.6 1.3 %deposit.1 = (f32[4,128]{1,0:T(4,128)S(1)}, f32[112,128]{1,0:T(8,128)S(1)}, f32[24,128]{1,0:T(8,128)S(1)}, f32[24,128]{1,0:T(8,128)S(1)}, f32[16,128]{1,0:T(8,12...) custom-call(s32[1]{0:T(128)} %bitcast.slab_ref, ...), custom_call_target="tpu_custom_call" | custom-call | tf_op jit(solution)/shard_map/deposit/pallas_call | solution.py:297
  1.9 1.8 %all-gather.1.both_ref = f32[2,4,128]{2,1,0:T(4,128)S(1)} all-gather(f32[1,4,128]{2,1,0:T(4,128)S(1)} %bitcast.3), channel_id=2, replica_groups={{1,0},{3,2},{5,4},{7,6},{9,8},{11,10},{13,12},{15,14},{17,16},{19,18},{..., dimensions={0}, use_global_device_ids=true | all-gather | bytes 6144 | tf_op jit(solution)/shard_map/all_gather | solution.py:315
  3.7 21.7 %all_to_all.10.got_ref = f32[16,4,128]{2,1,0:T(4,128)S(1)} all-to-all(f32[16,4,128]{2,1,0:T(4,128)S(1)} %repeat.1), channel_id=1, replica_groups={{16,18,20,22,24,26,28,30,0,2,4,6,8,10,12,14},{17,19,21,23,25,27,29,31,1..., dimensions={0} | all-to-all | bytes 65536 | tf_op jit(solution)/shard_map/all_to_all | solution.py:324
  25.4 12.0 %all_to_all.11.got_ref = f32[16,24,128]{2,1,0:T(8,128)S(1)} all-to-all(f32[16,24,128]{2,1,0:T(8,128)S(1)} %pack.1), channel_id=1, replica_groups={{320,352,256,288,448,480,384,416,64,96,0,32,192,224,128,160},{321,353,2..., dimensions={0} | all-to-all | bytes 393216 | tf_op jit(solution)/shard_map/all_to_all | solution.py:333
  37.3 1.3 %finish.1 = (f32[3,128]{1,0:T(4,128)}, f32[6,2816]{1,0:T(8,128)}) custom-call(s32[1]{0:T(128)} %bitcast.slab_ref, f32[16,24,128]{2,1,0:T(8,128)S(1)} %all_to_all.11.got_ref, f32[112,128]{1,0:T(8,128)S(1)} %get-tuple-element.15.dense_ref, f32[16,128]{1,0:T(8,128)S(1)} %get-tuple-element.16.near_ref, f32[16,128]{1,0:T(8,128)S(1)} %get-tuple-element.17.far_ref, ...), custom_call_target="tpu_custom_call" | custom-call | tf_op jit(solution)/shard_map/finish/pallas_call | solution.py:334
  (2 shorter events, 0.0 us)

commit v4 on v3

--- a/solution.py
+++ b/solution.py
@@ -151,10 +151,15 @@
             values[:, first * LANES:(first + group) * LANES], hot, (((1,), (1,)), ((), ())), preferred_element_type=F32
         )
     root = F32(1.0 / math.sqrt(fill))
-    moment_ref[0:1, :] = (total[0:1] + total[1:2] + total[2:3]) * root
-    moment_ref[1:2, :] = (total[3:4] + total[4:5] + total[5:6]) * root
-    moment_ref[2:3, :] = total[6:7] * F32(1.0 / fill)
-    moment_ref[3:4, :] = jnp.zeros((1, LANES), F32)
+    sums = jnp.concatenate([
+        (total[0:1] + total[1:2] + total[2:3]) * root,
+        (total[3:4] + total[4:5] + total[5:6]) * root,
+        total[6:7] * F32(1.0 / fill),
+        jnp.zeros((1, LANES), F32),
+    ], axis=0)
+    for slot in range(moment_ref.shape[0]):
+        for c in range(3):
+            moment_ref[slot, :, c * LANES:(c + 1) * LANES] = sums[c:c + 1]
 
 
 def make_payload(local, capacity, part_ref, index_ref, moving_ref, dense_ref, head_ref, tail_ref):
@@ -199,7 +204,8 @@
     head, tail = head_ref[...], tail_ref[...]
     for slot in range(slabs):
         out_ref[slot] = jnp.where((slot ^ FIRST_SLAB) < slab_ref[0], head, tail)
-        out_ref[slot, 0:3, :] = moments[0:3]
+        for c in range(3):
+            out_ref[slot, c:c + 1, :] = moments[:, c * LANES:(c + 1) * LANES]
 
 
 def finish_kernel(slabs, local, capacity, slab_ref, got_ref, dense_ref, near_ref, far_ref, trans_ref, long_ref,
@@ -296,7 +302,7 @@
 
     moments, dense, head, tail, near, far, trans, long, hop, coef = pl.pallas_call(
         functools.partial(deposit_kernel, slabs, local, capacity, fill),
-        out_shape=[shape_of(4, LANES), shape_of(7 * tiles, LANES), shape_of(ROWS, LANES), shape_of(ROWS, LANES),
+        out_shape=[shape_of(members, 1, 3 * LANES), shape_of(7 * tiles, LANES), shape_of(ROWS, LANES), shape_of(ROWS, LANES),
                    shape_of(16, LANES), shape_of(16, LANES), shape_of(LANES, LANES), shape_of(LANES, LANES),
                    shape_of(6, slabs, MODES), shape_of(4, slabs, MODES)],
         in_specs=specs(*"shhhhhh"),
@@ -312,16 +318,7 @@
     pairs = [[2 * z + 1, 2 * z] for z in range(chips)]
     rings = [[2 * ((z + FIRST_RING) % chips) + core for z in range(chips)] for core in range(2)]
     order = [slot ^ FIRST_SLAB for slot in range(slabs)]
-    both = lax.all_gather(moments, "pa", axis_index_groups=pairs)
-    repeated = pl.pallas_call(
-        repeat_kernel,
-        out_shape=pltpu.VMEM((chips, 4, LANES), F32),
-        in_specs=specs("v"),
-        out_specs=specs("v")[0],
-        compiler_params=SMALL,
-        name="repeat",
-    )(both)
-    gathered = lax.all_to_all(repeated, "pa", 0, 0, axis_index_groups=rings)
+    gathered = lax.all_to_all(moments, "pa", 0, 0, axis_index_groups=[[(2 * FIRST_RING + 1) ^ slot for slot in range(members)]])
     packed = pl.pallas_call(
         functools.partial(pack_kernel, slabs),
         out_shape=pltpu.VMEM((slabs, ROWS, LANES), F32),

time: 38.8 us -> 37.7 us (0.972)
  blocking collectives: 35.4 us -> 34.2 us
    all_gather x1 -> x0, blocking collectives: 1.78 us -> none  [body(): both = lax.all_gather(moments, 'pa', axis_index_groups=pairs)]
    all_to_all x1, blocking collectives: 21.7 us -> 22.2 us  [body(): lax.all_to_all(moments, 'pa', 0, 0, axis_index_groups=[[2 * FIRST_RING +...]
where the time goes in v4:
time: 37.7 us; the launch traced here: 37.4 us
  blocking collectives  34.2 us (91%)
  Pallas kernels  2.63 us (7%)
  between operations  0.65 us (2%)
    all_to_all x1, blocking collectives, body(): lax.all_to_all(moments, 'pa', 0, 0, axis_index_groups=[[2 * FIRST_RING +...  22.2 us
    all_to_all x1, blocking collectives, body(): everyone = lax.all_to_all(packed, 'gz', 0, 0, axis_index_groups=[order])  12 us
    pallas_call x1, Pallas kernels, body(): pl.pallas_call(functools.partial(deposit_kernel, slabs, local, capacity,...  1.29 us
    pallas_call x1, Pallas kernels, body(): pl.pallas_call(functools.partial(finish_kernel, slabs, local, capacity),...  1.29 us

profile of v4, /device:TPU:4, one launch (start us, length us, event | category | flops | bytes accessed | tf_op | source)
XLA Modules:
  0.0 37.4 jit_solution(9181512014566802235)
XLA Ops:
  0.6 1.3 %deposit.1 = (f32[32,1,384]{2,1,0:T(1,128)S(1)}, f32[112,128]{1,0:T(8,128)S(1)}, f32[24,128]{1,0:T(8,128)S(1)}, f32[24,128]{1,0:T(8,128)S(1)}, f32[16,128]{1,0:T...) custom-call(s32[1]{0:T(128)} %bitcast.slab_ref, ...), custom_call_target="tpu_custom_call" | custom-call | tf_op jit(solution)/shard_map/deposit/pallas_call | solution.py:303
  1.9 22.2 %all_to_all.10.got_ref = f32[32,1,384]{2,1,0:T(1,128)S(1)} all-to-all(f32[32,1,384]{2,1,0:T(1,128)S(1)} %get-tuple-element.12), channel_id=1, replica_groups={{17,16,19,18,21,20,23,22,25,24,27,26,29,28,31,30,1,0,3,2,5,4,7,6,9,8,11..., dimensions={0} | all-to-all | bytes 98304 | tf_op jit(solution)/shard_map/all_to_all | solution.py:321
  24.2 12.0 %all_to_all.11.got_ref = f32[16,24,128]{2,1,0:T(8,128)S(1)} all-to-all(f32[16,24,128]{2,1,0:T(8,128)S(1)} %pack.1), channel_id=1, replica_groups={{320,352,256,288,448,480,384,416,64,96,0,32,192,224,128,160},{321,353,2..., dimensions={0} | all-to-all | bytes 393216 | tf_op jit(solution)/shard_map/all_to_all | solution.py:330
  36.2 1.3 %finish.1 = (f32[3,128]{1,0:T(4,128)}, f32[6,2816]{1,0:T(8,128)}) custom-call(s32[1]{0:T(128)} %bitcast.slab_ref, f32[16,24,128]{2,1,0:T(8,128)S(1)} %all_to_all.11.got_ref, f32[112,128]{1,0:T(8,128)S(1)} %get-tuple-element.15.dense_ref, f32[16,128]{1,0:T(8,128)S(1)} %get-tuple-element.16.near_ref, f32[16,128]{1,0:T(8,128)S(1)} %get-tuple-element.17.far_ref, ...), custom_call_target="tpu_custom_call" | custom-call | tf_op jit(solution)/shard_map/finish/pallas_call | solution.py:331
  (1 shorter events, 0.0 us)

commit v5 on v4

--- a/solution.py
+++ b/solution.py
@@ -19,7 +19,8 @@
 SIN_TERMS = (6.2831854820251465, -41.34170150756836, 81.60513305664062, -76.70301818847656,
              42.02592849731445, -14.899847984313965, 3.238137722015381)
 SMALL = pltpu.CompilerParams(vmem_limit_bytes=4 << 20)
-FIRST_RING = 8
+FIRST_MEMBER = 17
+CUTS = (8, 22)
 FIRST_SLAB = 10
 INV_TWO_PI = 0.15915494309189535
 TURN_PARTS = (6.28125, 1.93500518798828125e-3, 3.0199159819567529e-7)
@@ -63,14 +64,14 @@
 
 
 def spread(read, shape, axis):
-    where = lax.broadcasted_iota(jnp.int32, shape, axis)
+    where = lax.broadcasted_iota(jnp.int32, shape, axis) % MODES
     total = jnp.zeros(shape, F32)
     for mode in range(MODES):
         total = jnp.where(where == mode, read(mode), total)
     return total
 
 
-def make_tables(slabs, width, slab_ref, decay_ref, freq_ref, amp_ref, near_ref, far_ref, trans_ref, long_ref, hop_ref, coef_ref):
+def make_tables(slabs, width, slab_ref, decay_ref, freq_ref, amp_ref, near_ref, far_ref, trans_ref, long_ref, mix_ref):
     shape = (MODES, LANES)
     scale = F32(1.0 / (slabs * width))
     damping = spread(lambda m: decay_ref[m], shape, 0) * scale
@@ -80,9 +81,9 @@
     near = powers(damping, freq, distance)
     far = powers(damping, freq, F32(width) - distance)
     near_ref[0:8, :] = near[0]
-    near_ref[8:16, :] = near[1]
-    far_ref[0:8, :] = far[0]
-    far_ref[8:16, :] = far[1]
+    near_ref[8:16, :] = -near[1]
+    for block, half in enumerate((0, 1, 1, 0)):
+        far_ref[8 * block:8 * block + 8, :] = far[half]
     norm_trans = jnp.sqrt(2.0 * damping)
     norm_long = jnp.sqrt(damping * damping + freq * freq)
     wave_trans = jnp.sum(norm_trans * (amps[0] * near[0] - amps[1] * near[1]), axis=0, keepdims=True)
@@ -93,16 +94,14 @@
         shifted = pltpu.roll(jnp.broadcast_to(wave, square), 0, 1, stride=1, stride_axis=0)
         ref[...] = jnp.where(later, shifted, F32(0.0))
 
-    small = (slabs, MODES)
+    small = (slabs, 2 * MODES)
     damping = spread(lambda m: decay_ref[m], small, 1) * scale
     freq = spread(lambda m: freq_ref[m], small, 1)
     amps = [spread(functools.partial(lambda row, m: amp_ref[row, m], row), small, 1) for row in range(4)]
     norm_trans = jnp.sqrt(2.0 * damping)
     norm_long = jnp.sqrt(damping * damping + freq * freq)
-    coef_ref[0] = amps[0] * norm_trans
-    coef_ref[1] = amps[1] * norm_trans
-    coef_ref[2] = amps[2] * norm_long
-    coef_ref[3] = amps[3] * norm_long
+    coefs = (amps[0] * norm_trans, amps[1] * norm_trans), (amps[2] * norm_long, amps[3] * norm_long)
+    sign = jnp.where(lax.broadcasted_iota(jnp.int32, small, 1) < MODES, F32(-1.0), F32(1.0))
     step = powers(damping, freq, jnp.full(small, width, F32))
     ladder = [step]
     while 2 ** len(ladder) < slabs:
@@ -115,9 +114,10 @@
             longer = complex_mul(weight, factor)
             taken = (hops & (1 << bit)) != 0
             weight = tuple(jnp.where(taken, b, a) for a, b in zip(weight, longer))
-        ahead = hops >= 0
-        hop_ref[2 * index] = jnp.where(ahead, weight[0], F32(0.0))
-        hop_ref[2 * index + 1] = jnp.where(ahead, weight[1], F32(0.0))
+        for kind, coef in enumerate(coefs):
+            mixed = complex_mul(weight, coef)
+            mix_ref[4 * index + 2 * kind] = jnp.where(hops >= 0, mixed[0], F32(0.0))
+            mix_ref[4 * index + 2 * kind + 1] = jnp.where(hops >= 0, sign * mixed[1], F32(0.0))
 
 
 def fetch(sources, targets, sems):
@@ -183,18 +183,12 @@
 
 
 def deposit_kernel(slabs, local, capacity, fill, slab_ref, part_hbm, index_hbm, moving_hbm, decay_hbm, freq_hbm, amp_hbm, *refs):
-    outs, (part_ref, index_ref, moving_ref, decay_ref, freq_ref, amp_ref, sems) = refs[:10], refs[10:]
+    outs, (part_ref, index_ref, moving_ref, decay_ref, freq_ref, amp_ref, sems) = refs[:9], refs[9:]
     fetch((part_hbm, index_hbm, moving_hbm, decay_hbm, freq_hbm, amp_hbm),
           (part_ref, index_ref, moving_ref, decay_ref, freq_ref, amp_ref), sems)
     deposit(local, fill, part_ref, index_ref, outs[0])
     make_payload(local, capacity, part_ref, index_ref, moving_ref, *outs[1:4])
     make_tables(slabs, LANES, slab_ref, decay_ref, freq_ref, amp_ref, *outs[4:])
-
-
-def repeat_kernel(both_ref, out_ref):
-    total = both_ref[0] + both_ref[1]
-    for slot in range(out_ref.shape[0]):
-        out_ref[slot] = total
 
 
 def pack_kernel(slabs, slab_ref, got_ref, head_ref, tail_ref, out_ref):
@@ -208,29 +202,24 @@
             out_ref[slot, c:c + 1, :] = moments[:, c * LANES:(c + 1) * LANES]
 
 
-def finish_kernel(slabs, local, capacity, slab_ref, got_ref, dense_ref, near_ref, far_ref, trans_ref, long_ref,
-                  hop_ref, coef_ref, kick_ref, out_ref, work_ref, done_ref):
+def finish_kernel(slabs, local, capacity, slab_ref, got_ref, dense_ref, near_ref, far_ref, trans_ref, long_ref, mix_ref, kick_hbm, out_hbm, work_ref, done_ref, kick_ref, out_ref, sems):
     tiles = local // LANES
     edge = capacity // LANES
     slab = slab_ref[0]
     nt = (((1,), (1,)), ((), ()))
     moments = jnp.concatenate([got_ref[:, c, :] for c in range(3)], axis=0)
-    sum_re = lax.dot_general(moments, far_ref[0:8, :], nt, precision=HIGH, preferred_element_type=F32)
-    sum_im = lax.dot_general(moments, far_ref[8:16, :], nt, precision=HIGH, preferred_element_type=F32)
-    line = lax.broadcasted_iota(jnp.int32, (ROWS, MODES), 0)
-    carry_re = jnp.zeros((ROWS, MODES), F32)
-    carry_im = jnp.zeros((ROWS, MODES), F32)
+    sums = lax.dot_general(moments, far_ref[0:16, :], nt, precision=HIGH, preferred_element_type=F32)
+    swapped = lax.dot_general(moments, far_ref[16:32, :], nt, precision=HIGH, preferred_element_type=F32)
+    line = lax.broadcasted_iota(jnp.int32, (ROWS, 2 * MODES), 0)
+    carry = jnp.zeros((ROWS, 2 * MODES), F32)
     for index in range(3):
-        weight = hop_ref[2 * index], hop_ref[2 * index + 1]
         for c in range(3):
-            part = complex_mul(weight, (sum_re[c * slabs:(c + 1) * slabs], sum_im[c * slabs:(c + 1) * slabs]))
-            part = complex_mul(part, (coef_ref[0], coef_ref[1]) if c < 2 else (coef_ref[2], coef_ref[3]))
-            here = line == 8 * index + c
-            carry_re = jnp.where(here, jnp.sum(part[0], axis=0, keepdims=True), carry_re)
-            carry_im = jnp.where(here, jnp.sum(part[1], axis=0, keepdims=True), carry_im)
+            mix = 4 * index + (2 if c == 2 else 0)
+            rows = slice(c * slabs, (c + 1) * slabs)
+            part = mix_ref[mix] * sums[rows] + mix_ref[mix + 1] * swapped[rows]
+            carry = jnp.where(line == 8 * index + c, jnp.sum(part, axis=0, keepdims=True), carry)
     plain = (((1,), (0,)), ((), ()))
-    incoming = lax.dot_general(carry_re, near_ref[0:8, :], plain, precision=HIGH, preferred_element_type=F32) - lax.dot_general(
-        carry_im, near_ref[8:16, :], plain, precision=HIGH, preferred_element_type=F32)
+    incoming = lax.dot_general(carry, near_ref[...], plain, precision=HIGH, preferred_element_type=F32)
     ahead = jnp.maximum(slab - 1, 0) ^ FIRST_SLAB
     behind = jnp.minimum(slab + 1, slabs - 1) ^ FIRST_SLAB
     near_moments = jnp.concatenate([got_ref[ahead, 0:8, :], got_ref[slab ^ FIRST_SLAB, 0:8, :], got_ref[behind, 0:8, :]], axis=0)
@@ -239,6 +228,8 @@
     wide = lax.broadcasted_iota(jnp.int32, (ROWS, LANES), 0)
     kicks = jnp.where(wide % 8 == 2, by_long, by_trans) + incoming
     kick_ref[...] = kicks[8:11]
+    copies = [pltpu.make_async_copy(kick_ref, kick_hbm, sems.at[0])]
+    copies[0].start()
 
     for q in range(6):
         work_ref[q * ROWS:q * ROWS + edge, :] = got_ref[behind, edge * (q + 1):edge * (q + 2), :]
@@ -276,6 +267,12 @@
         done_ref[q * ROWS:(q + 1) * ROWS, :] = jnp.where(kept, value, F32(0.0))
     for tile in range(tiles + 2 * edge):
         out_ref[:, tile * LANES:(tile + 1) * LANES] = done_ref[pl.ds(tile, 6, stride=ROWS), :]
+        if tile + 1 in CUTS:
+            piece = slice(([0] + [cut for cut in CUTS if cut <= tile])[-1] * LANES, (tile + 1) * LANES)
+            copies.append(pltpu.make_async_copy(out_ref.at[:, piece], out_hbm.at[:, piece], sems.at[len(copies)]))
+            copies[-1].start()
+    for copy in copies:
+        copy.wait()
 
 
 def specs(*kinds):
@@ -300,13 +297,13 @@
     slab = lax.axis_index("gz").astype(jnp.int32).reshape(1)
     index = slice_index.reshape(tiles, LANES)
 
-    moments, dense, head, tail, near, far, trans, long, hop, coef = pl.pallas_call(
+    moments, dense, head, tail, near, far, trans, long, mix = pl.pallas_call(
         functools.partial(deposit_kernel, slabs, local, capacity, fill),
         out_shape=[shape_of(members, 1, 3 * LANES), shape_of(7 * tiles, LANES), shape_of(ROWS, LANES), shape_of(ROWS, LANES),
-                   shape_of(16, LANES), shape_of(16, LANES), shape_of(LANES, LANES), shape_of(LANES, LANES),
-                   shape_of(6, slabs, MODES), shape_of(4, slabs, MODES)],
+                   shape_of(16, LANES), shape_of(32, LANES), shape_of(LANES, LANES), shape_of(LANES, LANES),
+                   shape_of(12, slabs, 2 * MODES)],
         in_specs=specs(*"shhhhhh"),
-        out_specs=specs(*"vvvvvvvvvv"),
+        out_specs=specs(*"vvvvvvvvv"),
         scratch_shapes=[pltpu.VMEM((6, local), F32), pltpu.VMEM((tiles, LANES), jnp.int32), pltpu.SMEM((1, 1, 2), jnp.int32),
                         pltpu.SMEM((MODES,), F32), pltpu.SMEM((MODES,), F32), pltpu.SMEM((4, MODES), F32),
                         pltpu.SemaphoreType.DMA((6,))],
@@ -314,14 +311,11 @@
         name="deposit",
     )(slab, *[stay(array) for array in (particles, index, moving, decay_rate, wake_freq, wake_amp)])
 
-    chips = members // 2
-    pairs = [[2 * z + 1, 2 * z] for z in range(chips)]
-    rings = [[2 * ((z + FIRST_RING) % chips) + core for z in range(chips)] for core in range(2)]
     order = [slot ^ FIRST_SLAB for slot in range(slabs)]
-    gathered = lax.all_to_all(moments, "pa", 0, 0, axis_index_groups=[[(2 * FIRST_RING + 1) ^ slot for slot in range(members)]])
+    gathered = lax.all_to_all(moments, "pa", 0, 0, axis_index_groups=[[FIRST_MEMBER ^ slot for slot in range(members)]])
     packed = pl.pallas_call(
         functools.partial(pack_kernel, slabs),
-        out_shape=pltpu.VMEM((slabs, ROWS, LANES), F32),
+        out_shape=shape_of(slabs, ROWS, LANES),
         in_specs=specs(*"svvv"),
         out_specs=specs("v")[0],
         compiler_params=SMALL,
@@ -331,12 +325,13 @@
     return pl.pallas_call(
         functools.partial(finish_kernel, slabs, local, capacity),
         out_shape=[shape_of(3, LANES), shape_of(6, local + 2 * capacity)],
-        in_specs=specs(*"svvvvvvvv"),
-        out_specs=specs(*"vv"),
-        scratch_shapes=[pltpu.VMEM((7 * ROWS, LANES), F32), pltpu.VMEM((6 * ROWS, LANES), F32)],
+        in_specs=specs(*"svvvvvvv"),
+        out_specs=specs(*"hh"),
+        scratch_shapes=[pltpu.VMEM((7 * ROWS, LANES), F32), pltpu.VMEM((6 * ROWS, LANES), F32), pltpu.VMEM((3, LANES), F32),
+                        pltpu.VMEM((6, local + 2 * capacity), F32), pltpu.SemaphoreType.DMA((1 + len(CUTS),))],
         compiler_params=SMALL,
         name="finish",
-    )(slab, everyone, dense, near, far, trans, long, hop, coef)
+    )(slab, everyone, dense, near, far, trans, long, mix)
 
 
 def solution(mesh):

time: 37.7 us -> 37.6 us (level)
  no operation moved by 1% of the time
where the time goes in v5:
time: 37.6 us; the launch traced here: 37.4 us
  blocking collectives  34.2 us (91%)
  Pallas kernels  2.6 us (7%)
  between operations  0.65 us (2%)
    all_to_all x1, blocking collectives, body(): lax.all_to_all(moments, 'pa', 0, 0, axis_index_groups=[[FIRST_MEMBER ^ sl...  22.2 us
    all_to_all x1, blocking collectives, body(): everyone = lax.all_to_all(packed, 'gz', 0, 0, axis_index_groups=[order])  12 us
    pallas_call x1, Pallas kernels, body(): pl.pallas_call(functools.partial(deposit_kernel, slabs, local, capacity,...  1.31 us
    pallas_call x1, Pallas kernels, body(): pl.pallas_call(functools.partial(finish_kernel, slabs, local, capacity),...  1.24 us

profile of v5, /device:TPU:4, one launch (start us, length us, event | category | flops | bytes accessed | tf_op | source)
XLA Modules:
  0.0 37.4 jit_solution(2390470377884744890)
XLA Ops:
  0.6 1.3 %deposit.1 = (f32[32,1,384]{2,1,0:T(1,128)S(1)}, f32[112,128]{1,0:T(8,128)S(1)}, f32[24,128]{1,0:T(8,128)S(1)}, f32[24,128]{1,0:T(8,128)S(1)}, f32[16,128]{1,0:T...) custom-call(s32[1]{0:T(128)} %bitcast.slab_ref, ...), custom_call_target="tpu_custom_call" | custom-call | tf_op jit(solution)/shard_map/deposit/pallas_call | solution.py:300
  2.0 22.2 %all_to_all.10.got_ref = f32[32,1,384]{2,1,0:T(1,128)S(1)} all-to-all(f32[32,1,384]{2,1,0:T(1,128)S(1)} %get-tuple-element.11), channel_id=1, replica_groups={{17,16,19,18,21,20,23,22,25,24,27,26,29,28,31,30,1,0,3,2,5,4,7,6,9,8,11..., dimensions={0} | all-to-all | bytes 98304 | tf_op jit(solution)/shard_map/all_to_all | solution.py:315
  24.2 12.0 %all_to_all.11.got_ref = f32[16,24,128]{2,1,0:T(8,128)S(1)} all-to-all(f32[16,24,128]{2,1,0:T(8,128)S(1)} %pack.1), channel_id=1, replica_groups={{320,352,256,288,448,480,384,416,64,96,0,32,192,224,128,160},{321,353,2..., dimensions={0} | all-to-all | bytes 393216 | tf_op jit(solution)/shard_map/all_to_all | solution.py:324
  36.2 1.2 %finish.1 = (f32[3,128]{1,0:T(4,128)}, f32[6,2816]{1,0:T(8,128)}) custom-call(s32[1]{0:T(128)} %bitcast.slab_ref, f32[16,24,128]{2,1,0:T(8,128)S(1)} %all_to_all.11.got_ref, f32[112,128]{1,0:T(8,128)S(1)} %get-tuple-element.14.dense_ref, f32[16,128]{1,0:T(8,128)S(1)} %get-tuple-element.15.near_ref, f32[32,128]{1,0:T(8,128)S(1)} %get-tuple-element.16.far_ref, ...), custom_call_target="tpu_custom_call" | custom-call | tf_op jit(solution)/shard_map/finish/pallas_call | solution.py:325
  (1 shorter events, 0.0 us)

commit v6 on v5

--- a/solution.py
+++ b/solution.py
@@ -71,7 +71,7 @@
     return total
 
 
-def make_tables(slabs, width, slab_ref, decay_ref, freq_ref, amp_ref, near_ref, far_ref, trans_ref, long_ref, mix_ref):
+def make_tables(slabs, width, slab_ref, decay_ref, freq_ref, amp_ref, near_ref, far_ref, local_ref, mix_ref):
     shape = (MODES, LANES)
     scale = F32(1.0 / (slabs * width))
     damping = spread(lambda m: decay_ref[m], shape, 0) * scale
@@ -80,33 +80,33 @@
     distance = lax.broadcasted_iota(jnp.int32, shape, 1).astype(F32)
     near = powers(damping, freq, distance)
     far = powers(damping, freq, F32(width) - distance)
-    near_ref[0:8, :] = near[0]
-    near_ref[8:16, :] = -near[1]
     for block, half in enumerate((0, 1, 1, 0)):
         far_ref[8 * block:8 * block + 8, :] = far[half]
+        near_ref[8 * block:8 * block + 8, :] = near[0] if block % 2 == 0 else -near[1]
     norm_trans = jnp.sqrt(2.0 * damping)
     norm_long = jnp.sqrt(damping * damping + freq * freq)
     wave_trans = jnp.sum(norm_trans * (amps[0] * near[0] - amps[1] * near[1]), axis=0, keepdims=True)
     wave_long = jnp.sum(norm_long * (amps[2] * near[0] - amps[3] * near[1]), axis=0, keepdims=True)
     square = (LANES, LANES)
     later = lax.broadcasted_iota(jnp.int32, square, 1) > lax.broadcasted_iota(jnp.int32, square, 0)
-    for wave, ref in ((wave_trans, trans_ref), (wave_long, long_ref)):
+    for kind, wave in enumerate((wave_trans, wave_long)):
         shifted = pltpu.roll(jnp.broadcast_to(wave, square), 0, 1, stride=1, stride_axis=0)
-        ref[...] = jnp.where(later, shifted, F32(0.0))
-
-    small = (slabs, 2 * MODES)
+        local_ref[:, kind * LANES:(kind + 1) * LANES] = jnp.where(later, shifted, F32(0.0))
+
+    small = (slabs, 4 * MODES)
     damping = spread(lambda m: decay_ref[m], small, 1) * scale
     freq = spread(lambda m: freq_ref[m], small, 1)
     amps = [spread(functools.partial(lambda row, m: amp_ref[row, m], row), small, 1) for row in range(4)]
     norm_trans = jnp.sqrt(2.0 * damping)
     norm_long = jnp.sqrt(damping * damping + freq * freq)
     coefs = (amps[0] * norm_trans, amps[1] * norm_trans), (amps[2] * norm_long, amps[3] * norm_long)
-    sign = jnp.where(lax.broadcasted_iota(jnp.int32, small, 1) < MODES, F32(-1.0), F32(1.0))
+    lane = lax.broadcasted_iota(jnp.int32, small, 1)
+    sign = jnp.where(lane < 3 * MODES, F32(-1.0), F32(1.0))
     step = powers(damping, freq, jnp.full(small, width, F32))
     ladder = [step]
     while 2 ** len(ladder) < slabs:
         ladder.append(complex_mul(ladder[-1], ladder[-1]))
-    source = lax.broadcasted_iota(jnp.int32, small, 0) ^ FIRST_SLAB
+    source = slab_of(lax.broadcasted_iota(jnp.int32, small, 0), slabs)
     for index in range(3):
         hops = slab_ref[0] + (index - 2) - source
         weight = (jnp.ones(small, F32), jnp.zeros(small, F32))
@@ -116,8 +116,16 @@
             weight = tuple(jnp.where(taken, b, a) for a, b in zip(weight, longer))
         for kind, coef in enumerate(coefs):
             mixed = complex_mul(weight, coef)
-            mix_ref[4 * index + 2 * kind] = jnp.where(hops >= 0, mixed[0], F32(0.0))
-            mix_ref[4 * index + 2 * kind + 1] = jnp.where(hops >= 0, sign * mixed[1], F32(0.0))
+            both = jnp.where(lane < 2 * MODES, mixed[0], sign * mixed[1])
+            mix_ref[2 * index + kind] = jnp.where(hops >= 0, both, F32(0.0))
+
+
+def slab_of(slot, slabs):
+    return (slot + FIRST_SLAB) % slabs
+
+
+def slot_of(slab, slabs):
+    return (slab + slabs - FIRST_SLAB) % slabs
 
 
 def fetch(sources, targets, sems):
@@ -151,15 +159,15 @@
             values[:, first * LANES:(first + group) * LANES], hot, (((1,), (1,)), ((), ())), preferred_element_type=F32
         )
     root = F32(1.0 / math.sqrt(fill))
-    sums = jnp.concatenate([
+    sums = (
         (total[0:1] + total[1:2] + total[2:3]) * root,
         (total[3:4] + total[4:5] + total[5:6]) * root,
         total[6:7] * F32(1.0 / fill),
-        jnp.zeros((1, LANES), F32),
-    ], axis=0)
-    for slot in range(moment_ref.shape[0]):
-        for c in range(3):
-            moment_ref[slot, :, c * LANES:(c + 1) * LANES] = sums[c:c + 1]
+    )
+    third = lax.broadcasted_iota(jnp.int32, (ROWS, LANES), 0) % 3
+    block = jnp.where(third == 0, sums[0], jnp.where(third == 1, sums[1], sums[2]))
+    for start in range(0, moment_ref.shape[0], ROWS):
+        moment_ref[start:start + ROWS, :] = block
 
 
 def make_payload(local, capacity, part_ref, index_ref, moving_ref, dense_ref, head_ref, tail_ref):
@@ -183,7 +191,7 @@
 
 
 def deposit_kernel(slabs, local, capacity, fill, slab_ref, part_hbm, index_hbm, moving_hbm, decay_hbm, freq_hbm, amp_hbm, *refs):
-    outs, (part_ref, index_ref, moving_ref, decay_ref, freq_ref, amp_ref, sems) = refs[:9], refs[9:]
+    outs, (part_ref, index_ref, moving_ref, decay_ref, freq_ref, amp_ref, sems) = refs[:8], refs[8:]
     fetch((part_hbm, index_hbm, moving_hbm, decay_hbm, freq_hbm, amp_hbm),
           (part_ref, index_ref, moving_ref, decay_ref, freq_ref, amp_ref), sems)
     deposit(local, fill, part_ref, index_ref, outs[0])
@@ -197,36 +205,32 @@
         moments = moments + got_ref[source]
     head, tail = head_ref[...], tail_ref[...]
     for slot in range(slabs):
-        out_ref[slot] = jnp.where((slot ^ FIRST_SLAB) < slab_ref[0], head, tail)
+        out_ref[slot] = jnp.where(slab_of(slot, slabs) < slab_ref[0], head, tail)
         for c in range(3):
             out_ref[slot, c:c + 1, :] = moments[:, c * LANES:(c + 1) * LANES]
 
 
-def finish_kernel(slabs, local, capacity, slab_ref, got_ref, dense_ref, near_ref, far_ref, trans_ref, long_ref, mix_ref, kick_hbm, out_hbm, work_ref, done_ref, kick_ref, out_ref, sems):
+def finish_kernel(slabs, local, capacity, slab_ref, got_ref, dense_ref, near_ref, far_ref, local_ref, mix_ref, kick_hbm, out_hbm, work_ref, done_ref, kick_ref, out_ref, sems):
     tiles = local // LANES
     edge = capacity // LANES
     slab = slab_ref[0]
     nt = (((1,), (1,)), ((), ()))
     moments = jnp.concatenate([got_ref[:, c, :] for c in range(3)], axis=0)
-    sums = lax.dot_general(moments, far_ref[0:16, :], nt, precision=HIGH, preferred_element_type=F32)
-    swapped = lax.dot_general(moments, far_ref[16:32, :], nt, precision=HIGH, preferred_element_type=F32)
-    line = lax.broadcasted_iota(jnp.int32, (ROWS, 2 * MODES), 0)
-    carry = jnp.zeros((ROWS, 2 * MODES), F32)
+    sums = lax.dot_general(moments, far_ref[...], nt, precision=HIGH, preferred_element_type=F32)
+    line = lax.broadcasted_iota(jnp.int32, (ROWS, 4 * MODES), 0)
+    carry = jnp.zeros((ROWS, 4 * MODES), F32)
     for index in range(3):
         for c in range(3):
-            mix = 4 * index + (2 if c == 2 else 0)
-            rows = slice(c * slabs, (c + 1) * slabs)
-            part = mix_ref[mix] * sums[rows] + mix_ref[mix + 1] * swapped[rows]
+            part = mix_ref[2 * index + (c == 2)] * sums[c * slabs:(c + 1) * slabs]
             carry = jnp.where(line == 8 * index + c, jnp.sum(part, axis=0, keepdims=True), carry)
     plain = (((1,), (0,)), ((), ()))
     incoming = lax.dot_general(carry, near_ref[...], plain, precision=HIGH, preferred_element_type=F32)
-    ahead = jnp.maximum(slab - 1, 0) ^ FIRST_SLAB
-    behind = jnp.minimum(slab + 1, slabs - 1) ^ FIRST_SLAB
-    near_moments = jnp.concatenate([got_ref[ahead, 0:8, :], got_ref[slab ^ FIRST_SLAB, 0:8, :], got_ref[behind, 0:8, :]], axis=0)
-    by_trans = lax.dot_general(near_moments, trans_ref[...], plain, precision=HIGH, preferred_element_type=F32)
-    by_long = lax.dot_general(near_moments, long_ref[...], plain, precision=HIGH, preferred_element_type=F32)
+    ahead = slot_of(jnp.maximum(slab - 1, 0), slabs)
+    behind = slot_of(jnp.minimum(slab + 1, slabs - 1), slabs)
+    near_moments = jnp.concatenate([got_ref[ahead, 0:8, :], got_ref[slot_of(slab, slabs), 0:8, :], got_ref[behind, 0:8, :]], axis=0)
+    local_kick = lax.dot_general(near_moments, local_ref[...], plain, precision=HIGH, preferred_element_type=F32)
     wide = lax.broadcasted_iota(jnp.int32, (ROWS, LANES), 0)
-    kicks = jnp.where(wide % 8 == 2, by_long, by_trans) + incoming
+    kicks = jnp.where(wide % 8 == 2, local_kick[:, LANES:], local_kick[:, :LANES]) + incoming
     kick_ref[...] = kicks[8:11]
     copies = [pltpu.make_async_copy(kick_ref, kick_hbm, sems.at[0])]
     copies[0].start()
@@ -297,13 +301,12 @@
     slab = lax.axis_index("gz").astype(jnp.int32).reshape(1)
     index = slice_index.reshape(tiles, LANES)
 
-    moments, dense, head, tail, near, far, trans, long, mix = pl.pallas_call(
+    moments, dense, head, tail, near, far, toeplitz, mix = pl.pallas_call(
         functools.partial(deposit_kernel, slabs, local, capacity, fill),
-        out_shape=[shape_of(members, 1, 3 * LANES), shape_of(7 * tiles, LANES), shape_of(ROWS, LANES), shape_of(ROWS, LANES),
-                   shape_of(16, LANES), shape_of(32, LANES), shape_of(LANES, LANES), shape_of(LANES, LANES),
-                   shape_of(12, slabs, 2 * MODES)],
+        out_shape=[shape_of(3 * members, LANES), shape_of(7 * tiles, LANES), shape_of(ROWS, LANES), shape_of(ROWS, LANES),
+                   shape_of(32, LANES), shape_of(32, LANES), shape_of(LANES, 2 * LANES), shape_of(6, slabs, 4 * MODES)],
         in_specs=specs(*"shhhhhh"),
-        out_specs=specs(*"vvvvvvvvv"),
+        out_specs=specs(*"vvvvvvvv"),
         scratch_shapes=[pltpu.VMEM((6, local), F32), pltpu.VMEM((tiles, LANES), jnp.int32), pltpu.SMEM((1, 1, 2), jnp.int32),
                         pltpu.SMEM((MODES,), F32), pltpu.SMEM((MODES,), F32), pltpu.SMEM((4, MODES), F32),
                         pltpu.SemaphoreType.DMA((6,))],
@@ -311,8 +314,8 @@
         name="deposit",
     )(slab, *[stay(array) for array in (particles, index, moving, decay_rate, wake_freq, wake_amp)])
 
-    order = [slot ^ FIRST_SLAB for slot in range(slabs)]
-    gathered = lax.all_to_all(moments, "pa", 0, 0, axis_index_groups=[[FIRST_MEMBER ^ slot for slot in range(members)]])
+    order = [slab_of(slot, slabs) for slot in range(slabs)]
+    gathered = lax.all_to_all(moments.reshape(members, 1, 3 * LANES), "pa", 0, 0, axis_index_groups=[[FIRST_MEMBER ^ slot for slot in range(members)]])
     packed = pl.pallas_call(
         functools.partial(pack_kernel, slabs),
         out_shape=shape_of(slabs, ROWS, LANES),
@@ -325,13 +328,13 @@
     return pl.pallas_call(
         functools.partial(finish_kernel, slabs, local, capacity),
         out_shape=[shape_of(3, LANES), shape_of(6, local + 2 * capacity)],
-        in_specs=specs(*"svvvvvvv"),
+        in_specs=specs(*"svvvvvv"),
         out_specs=specs(*"hh"),
         scratch_shapes=[pltpu.VMEM((7 * ROWS, LANES), F32), pltpu.VMEM((6 * ROWS, LANES), F32), pltpu.VMEM((3, LANES), F32),
                         pltpu.VMEM((6, local + 2 * capacity), F32), pltpu.SemaphoreType.DMA((1 + len(CUTS),))],
         compiler_params=SMALL,
         name="finish",
-    )(slab, everyone, dense, near, far, trans, long, mix)
+    )(slab, everyone, dense, near, far, toeplitz, mix)
 
 
 def solution(mesh):

time: 37.6 us -> 37.6 us (level)
  no operation moved by 1% of the time
where the time goes in v6:
time: 37.6 us; the launch traced here: 37.4 us
  blocking collectives  34.2 us (91%)
  Pallas kernels  2.54 us (7%)
  between operations  0.65 us (2%)
    all_to_all x1, blocking collectives, body(): lax.all_to_all(moments.reshape(members, 1, 3 * LANES), 'pa', 0, 0, axis_i...  22.2 us
    all_to_all x1, blocking collectives, body(): everyone = lax.all_to_all(packed, 'gz', 0, 0, axis_index_groups=[order])  12 us
    pallas_call x1, Pallas kernels, body(): pl.pallas_call(functools.partial(deposit_kernel, slabs, local, capacity,...  1.28 us
    pallas_call x1, Pallas kernels, body(): pl.pallas_call(functools.partial(finish_kernel, slabs, local, capacity),...  1.21 us

profile of v6, /device:TPU:4, one launch (start us, length us, event | category | flops | bytes accessed | tf_op | source)
XLA Modules:
  0.0 37.4 jit_solution(13012366431946647874)
XLA Ops:
  0.6 1.3 %deposit.1 = (f32[96,128]{1,0:T(8,128)S(1)}, f32[112,128]{1,0:T(8,128)S(1)}, f32[24,128]{1,0:T(8,128)S(1)}, f32[24,128]{1,0:T(8,128)S(1)}, f32[32,128]{1,0:T(8,1...) custom-call(s32[1]{0:T(128)} %bitcast.slab_ref, f32[6,2048]{1,0:T(8,128)} %part_hbm.1, ...), custom_call_target="tpu_custom_call" | custom-call | tf_op jit(solution)/shard_map/deposit/pallas_call | solution.py:304
  1.9 22.2 %all_to_all.10.got_ref = f32[32,1,384]{2,1,0:T(1,128)S(1)} all-to-all(f32[32,1,384]{2,1,0:T(1,128)S(1)} %bitcast.3), channel_id=1, replica_groups={{17,16,19,18,21,20,23,22,25,24,27,26,29,28,31,30,1,0,3,2,5,4,7,6,9,8,11..., dimensions={0} | all-to-all | bytes 98304 | tf_op jit(solution)/shard_map/all_to_all | solution.py:318
  24.2 12.0 %all_to_all.11.got_ref = f32[16,24,128]{2,1,0:T(8,128)S(1)} all-to-all(f32[16,24,128]{2,1,0:T(8,128)S(1)} %pack.1), channel_id=1, replica_groups={{320,352,384,416,448,480,0,32,64,96,128,160,192,224,256,288},{321,353,3..., dimensions={0} | all-to-all | bytes 393216 | tf_op jit(solution)/shard_map/all_to_all | solution.py:327
  36.1 1.2 %finish.1 = (f32[3,128]{1,0:T(4,128)}, f32[6,2816]{1,0:T(8,128)}) custom-call(s32[1]{0:T(128)} %bitcast.slab_ref, f32[16,24,128]{2,1,0:T(8,128)S(1)} %all_to_all.11.got_ref, f32[112,128]{1,0:T(8,128)S(1)} %get-tuple-element.13.dense_ref, f32[32,128]{1,0:T(8,128)S(1)} %get-tuple-element.14.near_ref, f32[32,128]{1,0:T(8,128)S(1)} %get-tuple-element.15.far_ref, ...), custom_call_target="tpu_custom_call" | custom-call | tf_op jit(solution)/shard_map/finish/pallas_call | solution.py:328
  (1 shorter events, 0.0 us)

commit v7 on v6

--- a/solution.py
+++ b/solution.py
@@ -291,6 +291,14 @@
     return jax.ShapeDtypeStruct(dims, F32)
 
 
+def outward(members):
+    chips = members // 2
+    ring = [FIRST_MEMBER // 2]
+    for step in range(1, chips // 2 + 1):
+        ring += [(ring[0] + step) % chips, (ring[0] - step) % chips]
+    return [2 * chip + core for chip in dict.fromkeys(ring) for core in (1, 0)]
+
+
 def body(particles, slice_index, moving, decay_rate, wake_freq, wake_amp):
     slabs = lax.axis_size("gz")
     members = lax.axis_size("pa")
@@ -315,7 +323,7 @@
     )(slab, *[stay(array) for array in (particles, index, moving, decay_rate, wake_freq, wake_amp)])
 
     order = [slab_of(slot, slabs) for slot in range(slabs)]
-    gathered = lax.all_to_all(moments.reshape(members, 1, 3 * LANES), "pa", 0, 0, axis_index_groups=[[FIRST_MEMBER ^ slot for slot in range(members)]])
+    gathered = lax.all_to_all(moments.reshape(members, 1, 3 * LANES), "pa", 0, 0, axis_index_groups=[outward(members)])
     packed = pl.pallas_call(
         functools.partial(pack_kernel, slabs),
         out_shape=shape_of(slabs, ROWS, LANES),

time: 37.6 us -> 37.5 us (level)
  no operation moved by 1% of the time
where the time goes in v7:
time: 37.5 us; the launch traced here: 37.3 us
  blocking collectives  34.1 us (91%)
  Pallas kernels  2.54 us (7%)
  between operations  0.65 us (2%)
    all_to_all x1, blocking collectives, body(): lax.all_to_all(moments.reshape(members, 1, 3 * LANES), 'pa', 0, 0, axis_i...  22.2 us
    all_to_all x1, blocking collectives, body(): everyone = lax.all_to_all(packed, 'gz', 0, 0, axis_index_groups=[order])  12 us
    pallas_call x1, Pallas kernels, body(): pl.pallas_call(functools.partial(deposit_kernel, slabs, local, capacity,...  1.28 us
    pallas_call x1, Pallas kernels, body(): pl.pallas_call(functools.partial(finish_kernel, slabs, local, capacity),...  1.21 us

profile of v7, /device:TPU:4, one launch (start us, length us, event | category | flops | bytes accessed | tf_op | source)
XLA Modules:
  0.0 37.3 jit_solution(8103478151359699781)
XLA Ops:
  0.6 1.3 %deposit.1 = (f32[96,128]{1,0:T(8,128)S(1)}, f32[112,128]{1,0:T(8,128)S(1)}, f32[24,128]{1,0:T(8,128)S(1)}, f32[24,128]{1,0:T(8,128)S(1)}, f32[32,128]{1,0:T(8,1...) custom-call(s32[1]{0:T(128)} %bitcast.slab_ref, f32[6,2048]{1,0:T(8,128)} %part_hbm.1, ...), custom_call_target="tpu_custom_call" | custom-call | tf_op jit(solution)/shard_map/deposit/pallas_call | solution.py:312
  1.9 22.2 %all_to_all.10.got_ref = f32[32,1,384]{2,1,0:T(1,128)S(1)} all-to-all(f32[32,1,384]{2,1,0:T(1,128)S(1)} %bitcast.3), channel_id=1, replica_groups={{17,16,19,18,15,14,21,20,13,12,23,22,11,10,25,24,9,8,27,26,7,6,29,28,5,..., dimensions={0} | all-to-all | bytes 98304 | tf_op jit(solution)/shard_map/all_to_all | solution.py:326
  24.2 12.0 %all_to_all.11.got_ref = f32[16,24,128]{2,1,0:T(8,128)S(1)} all-to-all(f32[16,24,128]{2,1,0:T(8,128)S(1)} %pack.1), channel_id=1, replica_groups={{320,352,384,416,448,480,0,32,64,96,128,160,192,224,256,288},{321,353,3..., dimensions={0} | all-to-all | bytes 393216 | tf_op jit(solution)/shard_map/all_to_all | solution.py:335
  36.1 1.2 %finish.1 = (f32[3,128]{1,0:T(4,128)}, f32[6,2816]{1,0:T(8,128)}) custom-call(s32[1]{0:T(128)} %bitcast.slab_ref, f32[16,24,128]{2,1,0:T(8,128)S(1)} %all_to_all.11.got_ref, f32[112,128]{1,0:T(8,128)S(1)} %get-tuple-element.13.dense_ref, f32[32,128]{1,0:T(8,128)S(1)} %get-tuple-element.14.near_ref, f32[32,128]{1,0:T(8,128)S(1)} %get-tuple-element.15.far_ref, ...), custom_call_target="tpu_custom_call" | custom-call | tf_op jit(solution)/shard_map/finish/pallas_call | solution.py:336
  (1 shorter events, 0.0 us)

commit v8 on v7

--- a/solution.py
+++ b/solution.py
@@ -19,7 +19,7 @@
 SIN_TERMS = (6.2831854820251465, -41.34170150756836, 81.60513305664062, -76.70301818847656,
              42.02592849731445, -14.899847984313965, 3.238137722015381)
 SMALL = pltpu.CompilerParams(vmem_limit_bytes=4 << 20)
-FIRST_MEMBER = 17
+FIRST_MEMBER = 19
 CUTS = (8, 22)
 FIRST_SLAB = 10
 INV_TWO_PI = 0.15915494309189535
@@ -150,7 +150,7 @@
     values = jnp.where(third == 0, high, jnp.where(third == 1, mid, low)).astype(bf)
     slot = lax.broadcasted_iota(jnp.int32, (LANES, LANES), 0)
     total = jnp.zeros((8, LANES), F32)
-    group = 2
+    group = 8
     for first in range(0, tiles, group):
         hot = jnp.concatenate(
             [(slot == index_ref[t:t + 1, :]).astype(F32).astype(bf) for t in range(first, first + group)], axis=1

time: 37.5 us -> 37.4 us (level)
  no operation moved by 1% of the time
where the time goes in v8:
time: 37.4 us; the launch traced here: 37.2 us
  blocking collectives  34 us (91%)
  Pallas kernels  2.54 us (7%)
  between operations  0.65 us (2%)
    all_to_all x1, blocking collectives, body(): lax.all_to_all(moments.reshape(members, 1, 3 * LANES), 'pa', 0, 0, axis_i...  22.1 us
    all_to_all x1, blocking collectives, body(): everyone = lax.all_to_all(packed, 'gz', 0, 0, axis_index_groups=[order])  12 us
    pallas_call x1, Pallas kernels, body(): pl.pallas_call(functools.partial(deposit_kernel, slabs, local, capacity,...  1.28 us
    pallas_call x1, Pallas kernels, body(): pl.pallas_call(functools.partial(finish_kernel, slabs, local, capacity),...  1.21 us

profile of v8, /device:TPU:4, one launch (start us, length us, event | category | flops | bytes accessed | tf_op | source)
XLA Modules:
  0.0 37.2 jit_solution(12045522734299710502)
XLA Ops:
  0.6 1.3 %deposit.1 = (f32[96,128]{1,0:T(8,128)S(1)}, f32[112,128]{1,0:T(8,128)S(1)}, f32[24,128]{1,0:T(8,128)S(1)}, f32[24,128]{1,0:T(8,128)S(1)}, f32[32,128]{1,0:T(8,1...) custom-call(s32[1]{0:T(128)} %bitcast.slab_ref, f32[6,2048]{1,0:T(8,128)} %part_hbm.1, ...), custom_call_target="tpu_custom_call" | custom-call | tf_op jit(solution)/shard_map/deposit/pallas_call | solution.py:312
  1.9 22.1 %all_to_all.10.got_ref = f32[32,1,384]{2,1,0:T(1,128)S(1)} all-to-all(f32[32,1,384]{2,1,0:T(1,128)S(1)} %bitcast.3), channel_id=1, replica_groups={{19,18,21,20,17,16,23,22,15,14,25,24,13,12,27,26,11,10,29,28,9,8,31,30,..., dimensions={0} | all-to-all | bytes 98304 | tf_op jit(solution)/shard_map/all_to_all | solution.py:326
  24.1 12.0 %all_to_all.11.got_ref = f32[16,24,128]{2,1,0:T(8,128)S(1)} all-to-all(f32[16,24,128]{2,1,0:T(8,128)S(1)} %pack.1), channel_id=1, replica_groups={{320,352,384,416,448,480,0,32,64,96,128,160,192,224,256,288},{321,353,3..., dimensions={0} | all-to-all | bytes 393216 | tf_op jit(solution)/shard_map/all_to_all | solution.py:335
  36.0 1.2 %finish.1 = (f32[3,128]{1,0:T(4,128)}, f32[6,2816]{1,0:T(8,128)}) custom-call(s32[1]{0:T(128)} %bitcast.slab_ref, f32[16,24,128]{2,1,0:T(8,128)S(1)} %all_to_all.11.got_ref, f32[112,128]{1,0:T(8,128)S(1)} %get-tuple-element.13.dense_ref, f32[32,128]{1,0:T(8,128)S(1)} %get-tuple-element.14.near_ref, f32[32,128]{1,0:T(8,128)S(1)} %get-tuple-element.15.far_ref, ...), custom_call_target="tpu_custom_call" | custom-call | tf_op jit(solution)/shard_map/finish/pallas_call | solution.py:336
  (1 shorter events, 0.0 us)

commit v9 on v8

--- a/solution.py
+++ b/solution.py
@@ -296,7 +296,8 @@
     ring = [FIRST_MEMBER // 2]
     for step in range(1, chips // 2 + 1):
         ring += [(ring[0] + step) % chips, (ring[0] - step) % chips]
-    return [2 * chip + core for chip in dict.fromkeys(ring) for core in (1, 0)]
+    rest = [2 * chip + core for chip in dict.fromkeys(ring) for core in (0, 1)]
+    return [FIRST_MEMBER] + [member for member in rest if member != FIRST_MEMBER]
 
 
 def body(particles, slice_index, moving, decay_rate, wake_freq, wake_amp):

time: 37.4 us -> 37.3 us (level)
  no operation moved by 1% of the time
where the time goes in v9:
time: 37.3 us; the launch traced here: 37.1 us
  blocking collectives  33.9 us (91%)
  Pallas kernels  2.54 us (7%)
  between operations  0.65 us (2%)
    all_to_all x1, blocking collectives, body(): lax.all_to_all(moments.reshape(members, 1, 3 * LANES), 'pa', 0, 0, axis_i...  22 us
    all_to_all x1, blocking collectives, body(): everyone = lax.all_to_all(packed, 'gz', 0, 0, axis_index_groups=[order])  12 us
    pallas_call x1, Pallas kernels, body(): pl.pallas_call(functools.partial(deposit_kernel, slabs, local, capacity,...  1.28 us
    pallas_call x1, Pallas kernels, body(): pl.pallas_call(functools.partial(finish_kernel, slabs, local, capacity),...  1.21 us

profile of v9, /device:TPU:4, one launch (start us, length us, event | category | flops | bytes accessed | tf_op | source)
XLA Modules:
  0.0 37.1 jit_solution(1949017790642720949)
XLA Ops:
  0.6 1.3 %deposit.1 = (f32[96,128]{1,0:T(8,128)S(1)}, f32[112,128]{1,0:T(8,128)S(1)}, f32[24,128]{1,0:T(8,128)S(1)}, f32[24,128]{1,0:T(8,128)S(1)}, f32[32,128]{1,0:T(8,1...) custom-call(s32[1]{0:T(128)} %bitcast.slab_ref, f32[6,2048]{1,0:T(8,128)} %part_hbm.1, ...), custom_call_target="tpu_custom_call" | custom-call | tf_op jit(solution)/shard_map/deposit/pallas_call | solution.py:313
  1.9 22.0 %all_to_all.10.got_ref = f32[32,1,384]{2,1,0:T(1,128)S(1)} all-to-all(f32[32,1,384]{2,1,0:T(1,128)S(1)} %bitcast.3), channel_id=1, replica_groups={{19,18,20,21,16,17,22,23,14,15,24,25,12,13,26,27,10,11,28,29,8,9,30,31,..., dimensions={0} | all-to-all | bytes 98304 | tf_op jit(solution)/shard_map/all_to_all | solution.py:327
  24.0 12.0 %all_to_all.11.got_ref = f32[16,24,128]{2,1,0:T(8,128)S(1)} all-to-all(f32[16,24,128]{2,1,0:T(8,128)S(1)} %pack.1), channel_id=1, replica_groups={{320,352,384,416,448,480,0,32,64,96,128,160,192,224,256,288},{321,353,3..., dimensions={0} | all-to-all | bytes 393216 | tf_op jit(solution)/shard_map/all_to_all | solution.py:336
  35.9 1.2 %finish.1 = (f32[3,128]{1,0:T(4,128)}, f32[6,2816]{1,0:T(8,128)}) custom-call(s32[1]{0:T(128)} %bitcast.slab_ref, f32[16,24,128]{2,1,0:T(8,128)S(1)} %all_to_all.11.got_ref, f32[112,128]{1,0:T(8,128)S(1)} %get-tuple-element.13.dense_ref, f32[32,128]{1,0:T(8,128)S(1)} %get-tuple-element.14.near_ref, f32[32,128]{1,0:T(8,128)S(1)} %get-tuple-element.15.far_ref, ...), custom_call_target="tpu_custom_call" | custom-call | tf_op jit(solution)/shard_map/finish/pallas_call | solution.py:337
  (1 shorter events, 0.0 us)
